TPU v7x, 128 devices: a whole 4x4x4 slice. The times are simulated.
128 devices in a mesh: lat: 32 (over z_lo, y, x), lon: 4 (over z_hi, core).
Axes of the slice: x: 4, y: 4, z: 4 (z_hi: 2, z_lo: 2; z = z_hi * 2 + z_lo), core: 2. Of those that a mesh axis runs over, the one named last changes fastest.
Arguments:
- vorticity: float32 [2, 1280, 2560], P(None, 'lat', 'lon'), may hold values from -46 to 46
- divergence: float32 [2, 1280, 2560], P(None, 'lat', 'lon'), may hold values from -46 to 46
- height: float32 [2, 1280, 2560], P(None, 'lat', 'lon'), may hold values from -46 to 46
- mean_geopot: float32 [2], replicated, may hold values from 0.5 to 8
Outputs:
- new_vorticity: float32 [2, 1280, 2560], P(None, 'lat', 'lon')
- new_divergence: float32 [2, 1280, 2560], P(None, 'lat', 'lon')
- new_height: float32 [2, 1280, 2560], P(None, 'lat', 'lon')
All inputs are finite; a program needn't handle non-finite values.
Results may differ from a plain program's by a relative error of at most 0.0017.
Values sent between devices are 32-bit elements; how exact they have to be, the bound alone decides.
No kernel may reach another device: no remote copies, remote signals or barrier semaphores. Data moves between devices by JAX's collectives and lax.ppermute only.
A program may use at most 320 MiB of HBM per device.

v0:
```python
import jax
import jax.numpy as jnp
from jax import lax
from jax.sharding import PartitionSpec as P

NLON = 2560
NLAT = 1280
MMAX = 1280


cap_sine = 0.5
filter_width = 64.0
diffusion = 4.0
renorm_big = 2.0**64
renorm_step = 64.0


def latitudes(row_index):
    colatitude = (4.0 * row_index + 3.0) * jnp.pi / (4.0 * NLAT + 2.0)
    shortfall = 1.0 / (8.0 * NLAT * NLAT) - 1.0 / (8.0 * NLAT * NLAT * NLAT)
    one_minus = shortfall + 2.0 * (1.0 - shortfall) * jnp.sin(0.5 * colatitude) ** 2
    one_plus = shortfall + 2.0 * (1.0 - shortfall) * jnp.cos(0.5 * colatitude) ** 2
    return (0.5 * (one_plus - one_minus), jnp.sqrt(one_minus * one_plus))


def sector_logs():
    sector_order = jnp.arange(1, MMAX, dtype=jnp.float32)
    log_terms = jnp.log2((2.0 * sector_order + 1.0) / (2.0 * sector_order))
    return jnp.concatenate([jnp.zeros((1,), jnp.float32), jnp.cumsum(log_terms)])


def fourier_table():
    points = jnp.arange(NLON, dtype=jnp.int32)
    wave_range = jnp.arange(MMAX, dtype=jnp.int32)
    phase_index = points[:, None] * wave_range[None, :] % NLON
    phase_angle = phase_index.astype(jnp.float32) * (2.0 * jnp.pi / NLON)
    return jnp.stack([jnp.cos(phase_angle), -jnp.sin(phase_angle)], axis=-1).reshape(NLON, 2 * MMAX)


def advance(recurrence, excess_degree, wave_col, cosine, wave_limit):
    previous, current, exponent = recurrence
    degree = wave_col + excess_degree
    first_row = excess_degree == 0
    growth = jnp.sqrt(
        (4.0 * degree * degree - 1.0)
        / jnp.maximum(excess_degree * (2.0 * wave_col + excess_degree), 1.0)
    )
    backward = jnp.sqrt(
        jnp.maximum((excess_degree - 1.0) * (2.0 * wave_col + excess_degree - 1.0), 0.0)
        / jnp.maximum(4.0 * (degree - 1.0) ** 2 - 1.0, 1.0)
    )
    following = growth * (cosine * current - backward * previous)
    too_large = jnp.abs(following) > renorm_big
    factor = jnp.where(too_large, 1.0 / renorm_big, 1.0)
    rescaled = (
        current * factor,
        following * factor,
        exponent + jnp.where(too_large, renorm_step, 0.0),
    )
    new_state = jax.tree.map(
        lambda kept, changed: jnp.where(first_row, kept, changed), recurrence, rescaled
    )
    row_value = new_state[1] * jnp.exp2(new_state[2])
    row_value = jnp.where(excess_degree < wave_limit, row_value, 0.0)
    return (new_state, row_value)


def legendre_blocks(wavenumbers, cumlog_part, cosine, sine_theta):
    wave_col = wavenumbers[:, None]
    log_start = -0.5 + 0.5 * cumlog_part[:, None] + wave_col * jnp.log2(sine_theta)[None, :]
    exponent = jnp.floor(log_start)
    leading = jnp.exp2(log_start - exponent)
    recurrence = (jnp.zeros_like(leading), leading, exponent)
    wave_limit = MMAX - wave_col
    cosine_row = cosine[None, :]
    legendre = jnp.zeros((wavenumbers.shape[0], MMAX, cosine.shape[0]), jnp.float32)
    anchor = jnp.zeros((), jnp.int32)

    def block_step(carry, block_index):
        state_now, table_now = carry
        row_list = []
        for offset in range(64):
            excess_degree = (block_index * 64 + offset).astype(jnp.float32)
            state_now, row_value = advance(
                state_now, excess_degree, wave_col, cosine_row, wave_limit
            )
            row_list.append(row_value)
        table_now = lax.dynamic_update_slice(
            table_now, jnp.stack(row_list, axis=1), (anchor, block_index * 64, anchor)
        )
        return ((state_now, table_now), None)

    (final_state, legendre), _ = lax.scan(
        block_step, (recurrence, legendre), jnp.arange(MMAX // 64, dtype=jnp.int32)
    )
    return legendre


def implicit(vort_part, div_part, height_part, degree, geopot):
    lap_ratio = degree * (degree + 1.0) / (MMAX * MMAX)
    coupling = jnp.sqrt(lap_ratio)
    damping = 1.0 / (1.0 + diffusion * lap_ratio * lap_ratio)
    div_new = (div_part + coupling * height_part) / (1.0 + geopot * coupling * coupling)
    height_new = height_part - geopot * coupling * div_new
    return (damping * vort_part, damping * div_new, damping * height_new)


def shards(vorticity, divergence, height, mean_geopot):
    n_lat = lax.axis_size("lat")
    n_lon = lax.axis_size("lon")
    lat_index = lax.axis_index("lat")
    lon_index = lax.axis_index("lon")
    levels = vorticity.shape[0]
    band_rows = vorticity.shape[1]
    sub_rows = band_rows // n_lon
    sectors = (
        lax.all_to_all(vorticity, "lon", split_axis=1, concat_axis=2, tiled=True),
        lax.all_to_all(divergence, "lon", split_axis=1, concat_axis=2, tiled=True),
        lax.all_to_all(height, "lon", split_axis=1, concat_axis=2, tiled=True),
    )
    stacked = jnp.stack(sectors)
    fourier = fourier_table()
    spectrum = (
        lax.dot_general(
            fourier,
            stacked,
            (((0,), (3,)), ((), ())),
            precision=lax.Precision.HIGHEST,
            preferred_element_type=jnp.float32,
        )
        / NLON
    )
    spectrum = spectrum.reshape(2 * MMAX, 3 * levels, sub_rows)
    waves_dev = MMAX // (n_lat * n_lon)
    columns = lax.all_to_all(spectrum, ("lat", "lon"), split_axis=0, concat_axis=2, tiled=True)
    row_index = jnp.arange(NLAT, dtype=jnp.int32)
    cosine, sine_theta = latitudes(row_index.astype(jnp.float32))
    weight = jnp.pi * sine_theta / (NLAT + 0.5)
    first_wave = (lat_index * n_lon + lon_index) * waves_dev
    wave_index = first_wave + jnp.arange(waves_dev, dtype=jnp.int32)
    wavenumbers = wave_index.astype(jnp.float32)
    excess = (
        jnp.maximum(wavenumbers[:, None] - MMAX * sine_theta[None, :] / cap_sine, 0.0)
        / filter_width
    )
    columns = (
        columns.reshape(waves_dev, 6 * levels, NLAT)
        * (weight[None, :] * jnp.exp(-0.5 * excess * excess))[:, None, :]
    )
    cumlog_part = lax.dynamic_slice_in_dim(sector_logs(), first_wave, waves_dev)
    legendre = legendre_blocks(wavenumbers, cumlog_part, cosine, sine_theta)
    spectral = lax.dot_general(
        columns,
        legendre,
        (((2,), (2,)), ((0,), (0,))),
        precision=lax.Precision.HIGHEST,
        preferred_element_type=jnp.float32,
    )
    spectral = spectral.reshape(waves_dev, 2, 3, levels, MMAX)
    degree = (wavenumbers[:, None] + jnp.arange(MMAX, dtype=jnp.float32)[None, :])[:, None, None, :]
    geopot = mean_geopot[None, None, :, None]
    new_v, new_d, new_h = implicit(
        spectral[:, :, 0], spectral[:, :, 1], spectral[:, :, 2], degree, geopot
    )
    updated = jnp.stack([new_v, new_d, new_h], axis=2).reshape(waves_dev, 6 * levels, MMAX)
    synthesis = lax.dot_general(
        updated,
        legendre,
        (((2,), (1,)), ((0,), (0,))),
        precision=lax.Precision.HIGHEST,
        preferred_element_type=jnp.float32,
    )
    doubling = jnp.where(wave_index == 0, 1.0, 2.0)
    synthesis = (synthesis * doubling[:, None, None]).reshape(2 * waves_dev, 3 * levels, NLAT)
    gathered = lax.all_to_all(synthesis, ("lat", "lon"), split_axis=2, concat_axis=0, tiled=True)
    result = lax.dot_general(
        gathered,
        fourier,
        (((0,), (1,)), ((), ())),
        precision=lax.Precision.HIGHEST,
        preferred_element_type=jnp.float32,
    )
    result = result.reshape(3, levels, sub_rows, NLON)
    pieces = (
        lax.all_to_all(result[0], "lon", split_axis=2, concat_axis=1, tiled=True),
        lax.all_to_all(result[1], "lon", split_axis=2, concat_axis=1, tiled=True),
        lax.all_to_all(result[2], "lon", split_axis=2, concat_axis=1, tiled=True),
    )
    return (pieces[0], pieces[1], pieces[2])


def solution(mesh):
    placed = (P(None, "lat", "lon"), P(None, "lat", "lon"), P(None, "lat", "lon"), P())
    return jax.shard_map(
        shards,
        mesh=mesh,
        in_specs=placed,
        out_specs=(P(None, "lat", "lon"), P(None, "lat", "lon"), P(None, "lat", "lon")),
        check_vma=False,
    )
```

profile of v0, /device:TPU:1, one launch (start us, length us, event | category | flops | bytes accessed | tf_op | source)
XLA Modules:
  0.0 1663.4 jit_solution(17525326497861117534)
XLA Ops:
  0.6 1.7 copy.113
  2.3 6.6 all-to-all-start.2
  9.0 54.7 %sine_negate_fusion = (f32[2560,1280,1]{1,0,2:T(8,128)}, f32[2560,1280,1]{1,0,2:T(8,128)}) fusion(), kind=kLoop, calls=%fused_computation.1360 | loop fusion | flops 32768000 | bytes 26214400 | tf_op jit(solution)/shard_map/neg | solution.py:37
  64.3 17.7 %pad_maximum_fusion = f32[2560,1280,2]{1,0,2:T(8,128)} fusion(f32[2560,1280,1]{1,0,2:T(8,128)} %get-tuple-element.1296, f32[2560,1280,1]{1,0,2:T(8,128)} %get-tuple-element.1297), kind=kLoop, calls=%fused_computation.1352 | loop fusion | flops 6553600 | bytes 52428800 | tf_op jit(solution)/shard_map/stack | solution.py:37
  82.9 4.8 all-to-all-start.1
  88.7 5.1 all-to-all-done.1
  93.8 4.7 all-to-all-start
  99.3 38.9 %copy.108 = f32[2560,1280,2]{0,2,1:T(2,128)} copy(f32[2560,1280,2]{1,0,2:T(8,128)} %pad_maximum_fusion) | data formatting | bytes 52428800 | tf_op jit(solution)/shard_map/stack | solution.py:37
  138.2 31.5 %reshape.4587 = f32[2560,2560]{0,1:T(8,128)} reshape(f32[2560,1280,2]{0,2,1:T(2,128)} %copy.108) | data formatting | bytes 52428800 | tf_op jit(solution)/shard_map/reshape | solution.py:37
  170.2 28.7 %fusion.656 = f32[2560,3,2,10]{0,3,2,1:T(8,128)S(1)} fusion(f32[2560,2560]{0,1:T(8,128)} %reshape.4587, f32[1,2,10,2560]{3,2,1,0:T(8,128)S(1)} %reshape.4919, f32[1,2,10,2560]{3,2,1,0:T(8,128)S(1)} %reshape.4918, f32[1,2,10,2560]{3,2,1,0:T(8,128)S(1)} %reshape.4917), kind=kOutput, calls=%fused_computation.1366 | convolution fusion | flops 4719052800 | bytes 27443200 | tf_op jit(solution)/shard_map/dot_general | solution.py:124
  198.9 5.5 copy.119
  204.3 8.5 reshape.4923
  212.9 9.9 all-to-all-start.3
  222.8 20.7 %broadcast_in_dim.1016.clone = f32[10,1280,1280]{2,1,0:T(8,128)} broadcast(f32[]{:T(128)} %constant.863.clone.1), dimensions={} | broadcast | bytes 65536004 | tf_op jit(solution)/shard_map/broadcast_in_dim | solution.py:76
  243.5 1170.4 %while.23 = (s32[]{:T(128)}, f32[10,1280]{1,0:T(8,128)S(1)}, f32[10,1280]{1,0:T(8,128)S(1)}, f32[10,1280]{1,0:T(8,128)S(1)}, f32[10,1280,1280]{2,1,0:T(8,128)}, ...) while((s32[]{:T(128)}, f32[10,1280]{1,0:T(8,128)S(1)}, ...), condition=%wide.region_3.4_spmd.clone.clone.clone.clone, body=%wide.region_2.3_spmd.clone.clone.clone.clone.sunk | while | flops 19717672 | bytes 36492556 | solution.py:93
  295.9 6.2 copy_dynamic-update-slice_fusion.2
  354.4 6.2 copy_dynamic-update-slice_fusion.2
  413.0 6.1 copy_dynamic-update-slice_fusion.2
  471.5 6.1 copy_dynamic-update-slice_fusion.2
  529.9 6.1 copy_dynamic-update-slice_fusion.2
  588.4 6.1 copy_dynamic-update-slice_fusion.2
  646.9 6.2 copy_dynamic-update-slice_fusion.2
  705.4 6.1 copy_dynamic-update-slice_fusion.2
  763.9 6.2 copy_dynamic-update-slice_fusion.2
  822.5 6.1 copy_dynamic-update-slice_fusion.2
  881.0 6.1 copy_dynamic-update-slice_fusion.2
  939.5 6.2 copy_dynamic-update-slice_fusion.2
  998.0 6.1 copy_dynamic-update-slice_fusion.2
  1056.5 6.1 copy_dynamic-update-slice_fusion.2
  1115.0 6.1 copy_dynamic-update-slice_fusion.2
  1173.5 6.2 copy_dynamic-update-slice_fusion.2
  1232.1 6.2 copy_dynamic-update-slice_fusion.2
  1290.7 6.1 copy_dynamic-update-slice_fusion.2
  1349.1 6.1 copy_dynamic-update-slice_fusion.2
  1407.6 6.1 copy_dynamic-update-slice_fusion.2
  1414.7 2.2 reduce.4
  1416.9 7.1 reshape.4924
  1424.0 11.6 copy.121
  1435.6 6.7 reshape.4589
  1442.4 58.3 %fusion.664 = f32[10,12,1280]{2,1,0:T(8,128)S(1)} fusion(f32[10,1280,1280]{2,1,0:T(8,128)} %get-tuple-element.647, f32[10,12,1280]{2,1,0:T(8,128)S(1)} %reshape.4589, f32[10,1280]{1,0:T(8,128)S(1)} %copy-done), kind=kOutput, calls=%fused_computation.1373 | convolution fusion | flops 2359449600 | bytes 66816000 | tf_op jit(solution)/shard_map/dot_general | solution.py:152
  1502.2 36.2 %convolution_multiply_fusion = f32[10,12,1280]{2,1,0:T(8,128)S(1)} fusion(f32[10,12,1280]{2,1,0:T(8,128)S(1)} %reshape.4593, f32[10,1280,1280]{2,1,0:T(8,128)} %get-tuple-element.647, f32[10]{0:T(128)S(1)} %compare_select_fusion), kind=kOutput, calls=%fused_computation.1367 | convolution fusion | flops 2359449600 | bytes 66764840 | tf_op jit(solution)/shard_map/dot_general | solution.py:166
  1538.5 3.3 copy.124
  1541.8 4.7 reshape.4925
  1546.5 24.6 %all_to_all.132 = f32[128,1,1200]{2,1,0:T(1,128)S(1)} all-to-all(f32[128,1,1200]{2,1,0:T(1,128)S(1)} %reshape.4925), channel_id=1, replica_groups=mesh['lat'=32,'lon'=4] {'lat','lon'}, dimensions={0} | all-to-all | bytes 1228800 | tf_op jit(solution)/shard_map/all_to_all | solution.py:175
  1571.1 2.2 reduce.5
  1573.3 3.8 reshape.4926
  1577.1 5.7 copy.151
  1582.8 4.9 reshape.4920
  1587.8 17.9 %fusion.646 = f32[6,10,2560]{2,1,0:T(8,128)S(1)} fusion(f32[2560,6,10]{0,2,1:T(8,128)S(1)} %reshape.4920, f32[2560,2560]{0,1:T(8,128)} %reshape.4587), kind=kOutput, calls=%fused_computation.1353 | convolution fusion | flops 4718592000 | bytes 27443200 | tf_op jit(solution)/shard_map/dot_general | solution.py:176
  1606.5 3.1 copy.129
  1609.6 4.8 reshape.4927
  1614.4 3.8 all-to-all-start.5
  1618.1 1.3 copy.132
  1619.4 4.8 reshape.4929
  1624.2 4.8 all-to-all-start.6
  1629.0 1.3 copy.135
  1630.3 4.8 reshape.4931
  1635.1 5.0 all-to-all-start.7
  1640.1 1.9 reduce.6
  1642.0 4.9 reshape.4928
  1648.9 1.2 reduce.7
  1650.1 3.9 reshape.4930
  1656.0 1.2 reduce.8
  1657.3 3.9 reshape.4932
  (3317 shorter events, 1040.5 us)
Async XLA Ops:
  2.3 80.6 %all-to-all-start.2 = ((f32[2,40,640]{2,0,1:T(2,128)}), f32[2,40,640]{2,0,1:T(2,128)S(1)}, u32[]{:S(2)}, u32[]{:S(2)}) async-start(f32[2,40,640]{2,0,1:T(2,128)} %copy.113), calls=%async_computation.2 | async-start | bytes 409600 | tf_op jit(solution)/shard_map/all_to_all | solution.py:119
  64.3 17.7 %copy-start.2 = (f32[2,40,640]{2,1,0:T(8,128)S(1)}, f32[2,40,640]{2,1,0:T(8,128)}, u32[]{:S(2)}) copy-start(f32[2,40,640]{2,1,0:T(8,128)} %param.7) | copy-start | bytes 614404
  64.3 23.5 %copy-start.3 = (f32[2,40,640]{2,1,0:T(8,128)S(1)}, f32[2,40,640]{2,1,0:T(8,128)}, u32[]{:S(2)}) copy-start(f32[2,40,640]{2,1,0:T(8,128)} %param.6) | copy-start | bytes 614404
  82.9 10.9 all-to-all-start.1
  93.8 76.2 %all-to-all-start = ((f32[2,40,640]{2,0,1:T(2,128)}), f32[2,40,640]{2,0,1:T(2,128)S(1)}, u32[]{:S(2)}, u32[]{:S(2)}) async-start(f32[2,40,640]{2,0,1:T(2,128)} %copy.109), calls=%async_computation | async-start | bytes 409600 | tf_op jit(solution)/shard_map/all_to_all | solution.py:117
  212.9 1201.2 %all-to-all-start.3 = ((f32[128,1,1200]{2,1,0:T(1,128)}), f32[128,1,1200]{2,1,0:T(1,128)S(1)}, u32[]{:S(2)}, u32[]{:S(2)}) async-start(f32[128,1,1200]{2,1,0:T(1,128)} %reshape.4923), calls=%async_computation.3 | async-start | bytes 1310720 | tf_op jit(solution)/shard_map/all_to_all | solution.py:135
  243.5 1170.5 %copy-start.4 = (f32[2]{0:T(128)S(1)}, f32[2]{0:T(128)}, u32[]{:S(2)}) copy-start(f32[2]{0:T(128)} %param.9) | copy-start | bytes 28
  1435.6 6.7 copy-start
  1442.4 58.7 %copy-start.1 = (f32[10,1280]{1,0:T(8,128)S(1)}, f32[10,1280]{1,0:T(8,128)}, u32[]{:S(2)}) copy-start(f32[10,1280]{1,0:T(8,128)} %get-tuple-element.1293) | copy-start | bytes 153604
  1614.4 9.8 all-to-all-start.5
  1624.2 10.9 all-to-all-start.6
  1635.1 20.9 %all-to-all-start.7 = ((f32[4,1,12800]{2,1,0:T(1,128)}), f32[4,1,12800]{2,1,0:T(1,128)S(1)}, u32[]{:S(2)}, u32[]{:S(2)}) async-start(f32[4,1,12800]{2,1,0:T(1,128)} %reshape.4931), calls=%async_computation.7 | async-start | bytes 409600 | tf_op jit(solution)/shard_map/all_to_all | solution.py:187
where the time goes:
time: 1670 us; the launch traced here: 1660 us
  other arithmetic  1100 us (66%)
  local copies, waits for them, and re-layouts  332 us (20%)
  matrix products  141 us (8%)
  starting transfers between devices  39.6 us (2%)
  blocking collectives  24.6 us (1%)
  loops' own time  20 us (1%)
    while x1260, other arithmetic  965 us
    dynamic_update_slice x20, local copies, waits for them, and re-layouts, block_step(): lax.dynamic_update_slice(table_now, jnp.stack(row_list, axis=1), (anchor,...  123 us
    dot_general x1, matrix products, shards(): lax.dot_general(columns, legendre, (((2,), (2,)), ((0,), (0,))), precisio...  58.3 us
    unnamed x26, local copies, waits for them, and re-layouts  56.7 us
    neg x1, other arithmetic, fourier_table(): -jnp.sin(phase_angle)  54.7 us
    another operation x1, local copies, waits for them, and re-layouts, fourier_table(): jnp.stack([jnp.cos(phase_angle), -jnp.sin(phase_angle)], axis=-1)  38.9 us
    dot_general x1, matrix products, shards(): lax.dot_general(updated, legendre, (((2,), (1,)), ((0,), (0,))), precisio...  36.2 us
  transfers between devices with their start and end apart: 7, of which 1 were waited for; matrix products, arithmetic and copies ran while one was open for 81% of the time, Pallas kernels for 0%

commit v1 on v0

v1 whole, which is shorter than its diff:
```python
import jax
import jax.numpy as jnp
import ml_dtypes
import numpy as np
from jax import lax
from jax.experimental import pallas as pl
from jax.experimental.pallas import tpu as pltpu
from jax.sharding import PartitionSpec as P

NLON = 2560
NLAT = 1280
MMAX = 1280
F32 = jnp.float32
BF16 = jnp.bfloat16
STEPS = 64
CHUNKS = MMAX // STEPS
TILES = 5
LANES = 128

cap_sine = 0.5
filter_width = 64.0
diffusion = 4.0
renorm_big = 2.0**64
renorm_step = 64.0


def split_np(values):
    values = np.asarray(values, np.float64).astype(np.float32)
    high = values.astype(ml_dtypes.bfloat16)
    low = (values - high.astype(np.float32)).astype(ml_dtypes.bfloat16)
    return high, low


def latitude_rows():
    rows = np.arange(NLAT // 2, dtype=np.float64)
    colatitude = (4.0 * rows + 3.0) * np.pi / (4.0 * NLAT + 2.0)
    shortfall = 1.0 / (8.0 * NLAT * NLAT) - 1.0 / (8.0 * NLAT * NLAT * NLAT)
    one_minus = shortfall + 2.0 * (1.0 - shortfall) * np.sin(0.5 * colatitude) ** 2
    one_plus = shortfall + 2.0 * (1.0 - shortfall) * np.cos(0.5 * colatitude) ** 2
    cosine = 0.5 * (one_plus - one_minus)
    sine = np.sqrt(one_minus * one_plus)
    weight = np.pi * sine / (NLAT + 0.5)
    log_sine = np.log2(sine)
    log_high = np.round(log_sine * 256.0) / 256.0
    log_low = log_sine - log_high
    table = np.stack([cosine, log_high, log_low, MMAX * sine / cap_sine, weight])
    lane = np.arange(NLAT // 2)
    order = 10 * (lane % 64) + lane // 64
    full = np.zeros((8, NLAT // 2), np.float32)
    full[:5] = table[:, order]
    return full


def sector_logs():
    order = np.arange(1, MMAX, dtype=np.float64)
    terms = np.log2((2.0 * order + 1.0) / (2.0 * order))
    return (-0.5 + 0.5 * np.concatenate([[0.0], np.cumsum(terms)])).astype(np.float32)


def gather_matrix():
    out = np.zeros((10, 3, 2, 2, 2, 256), np.float32)
    for u in range(10):
        for f in range(3):
            for q in range(2):
                for c in range(2):
                    for lev in range(2):
                        out[u, f, q, c, lev, q * 128 + c * 64 + (2 * f + lev) * 10 + u] = 1.0
    return out.reshape(240, 256).astype(ml_dtypes.bfloat16)


def fold_matrix():
    out = np.zeros((4, 128, 2, 128), np.float32)
    for src in range(64):
        out[0, src, :, src] = 1.0
        out[1, src, :, 64 + src] = 1.0
        out[2, 127 - src, 0, src] = 1.0
        out[2, 127 - src, 1, src] = -1.0
        out[3, 127 - src, 0, 64 + src] = 1.0
        out[3, 127 - src, 1, 64 + src] = -1.0
    return out.reshape(512, 256).astype(ml_dtypes.bfloat16)


def unfold_matrix():
    out = np.zeros((4, 64, 2, 128), np.float32)
    for row in range(64):
        out[0, row, :, row] = 1.0
        out[1, row, :, 64 + row] = 1.0
        out[2, row, 0, 63 - row] = 1.0
        out[2, row, 1, 63 - row] = -1.0
        out[3, row, 0, 127 - row] = 1.0
        out[3, row, 1, 127 - row] = -1.0
    return out.reshape(256, 256).astype(ml_dtypes.bfloat16)


def scatter_matrix():
    out = np.zeros((2, 2, 5, 8, 128), np.float32)
    for c in range(2):
        for h in range(2):
            for i in range(5):
                for f in range(3):
                    for lev in range(2):
                        out[c, h, i, 2 * f + lev, 40 * f + 4 * (5 * h + i) + 2 * c + lev] = 1.0
    return out.reshape(160, 128).astype(ml_dtypes.bfloat16)


def forward_matrix():
    angle = 2.0 * np.pi * (np.outer(np.arange(64), np.arange(128)) % 128) / 128.0
    table = np.concatenate([np.cos(angle), np.sin(angle)], axis=1) / NLON
    high, low = split_np(table)
    return np.concatenate([high, low], axis=0)


def inverse_matrix():
    angle = 2.0 * np.pi * (np.outer(np.arange(64), np.arange(128)) % 128) / 128.0
    cosine = np.cos(angle).reshape(2, 1, 32, 128)
    sine = np.sin(angle).reshape(2, 1, 32, 128)
    real_part = np.concatenate([cosine, sine], axis=-1)
    imag_part = np.concatenate([-sine, cosine], axis=-1)
    table = np.broadcast_to(np.stack([real_part, imag_part]), (2, 2, 4, 32, 256)).reshape(512, 256)
    high, low = split_np(table)
    return np.concatenate([high, low], axis=0)


def twiddles():
    angle = 2.0 * np.pi * np.outer(np.arange(20), np.arange(128)) / NLON
    return np.stack([np.cos(angle), np.sin(angle)], axis=1).reshape(40, 128).astype(np.float32)


def split(values):
    high = values.astype(BF16)
    return high, (values - high.astype(F32)).astype(BF16)


def dot(left, right):
    return lax.dot_general(left, right, (((1,), (0,)), ((), ())), preferred_element_type=F32)


def dot_t(left, right):
    return lax.dot_general(left, right, (((1,), (1,)), ((), ())), preferred_element_type=F32)


C1, C2 = float(np.cos(2 * np.pi / 5)), float(np.cos(4 * np.pi / 5))
S1, S2 = float(np.sin(2 * np.pi / 5)), float(np.sin(4 * np.pi / 5))


def pack_kernel(vort_ref, div_ref, height_ref, out_ref):
    for b in range(4):
        for f, ref in enumerate((vort_ref, div_ref, height_ref)):
            for lev in range(2):
                out_ref[b, pl.ds((2 * f + lev) * 10, 10), :] = ref[lev, pl.ds(10 * b, 10), :]
        out_ref[b, pl.ds(60, 4), :] = jnp.zeros((4, 640), F32)


def unpack_kernel(in_ref, vort_ref, div_ref, height_ref):
    for b in range(4):
        for f, ref in enumerate((vort_ref, div_ref, height_ref)):
            for lev in range(2):
                ref[lev, pl.ds(10 * b, 10), :] = in_ref[b, pl.ds((2 * f + lev) * 10, 10), :]


def forward_kernel(in_ref, twiddle_ref, table_ref, out_ref, z_ref):
    @pl.loop(0, 8)
    def _(group):
        rows = pl.ds(pl.multiple_of(group * 8, 8), 8)
        x = [in_ref[i2 // 5, rows, pl.ds((i2 % 5) * 128, 128)] for i2 in range(20)]
        parts = []
        for n4 in range(4):
            v = [x[(4 * n5 + 5 * n4) % 20] for n5 in range(5)]
            p1, p2 = v[1] + v[4], v[2] + v[3]
            q1, q2 = v[1] - v[4], v[2] - v[3]
            parts.append(
                (
                    (v[0] + p1 + p2, None),
                    (v[0] + C1 * p1 + C2 * p2, -(S1 * q1 + S2 * q2)),
                    (v[0] + C2 * p1 + C1 * p2, S1 * q2 - S2 * q1),
                )
            )
        y = {}
        zero = jnp.zeros_like(x[0])
        g = [parts[n4][0][0] for n4 in range(4)]
        y[0, 0] = (g[0] + g[2] + (g[1] + g[3]), zero)
        y[2, 0] = (g[0] + g[2] - (g[1] + g[3]), zero)
        y[1, 0] = (g[0] - g[2], g[3] - g[1])
        y[3, 0] = (g[0] - g[2], g[1] - g[3])
        for b5 in (1, 2):
            re = [parts[n4][b5][0] for n4 in range(4)]
            im = [parts[n4][b5][1] for n4 in range(4)]
            er, ei = re[0] + re[2], im[0] + im[2]
            odr, odi = re[1] + re[3], im[1] + im[3]
            dr, di = re[0] - re[2], im[0] - im[2]
            fr, fi = re[1] - re[3], im[1] - im[3]
            y[0, b5] = (er + odr, ei + odi)
            y[2, b5] = (er - odr, ei - odi)
            y[1, b5] = (dr + fi, di - fr)
            y[3, b5] = (dr - fi, di + fr)
        for b in range(20):
            if b % 5 <= 2:
                yr, yi = y[b % 4, b % 5]
            else:
                yr, yi = y[-b % 4, 5 - b % 5]
                yi = -yi
            tr = twiddle_ref[pl.ds(2 * b, 1), :]
            ti = twiddle_ref[pl.ds(2 * b + 1, 1), :]
            z_ref[b, rows, pl.ds(0, 128)] = yr * tr + yi * ti
            z_ref[b, rows, pl.ds(128, 128)] = yi * tr - yr * ti

    table = table_ref[...]
    for b in range(20):
        re = z_ref[b, :, pl.ds(0, 128)]
        im = z_ref[b, :, pl.ds(128, 128)]
        re_hi, re_lo = split(re)
        im_hi, im_lo = split(im)

        def both(real, imag):
            top = jnp.concatenate([real, imag], axis=1)
            return jnp.concatenate([top, jnp.concatenate([imag, -real], axis=1)], axis=0)

        first = dot_t(table, both(re_hi, im_hi))
        total = first[:64] + first[64:] + dot_t(table[:64], both(re_lo, im_lo))
        for h in range(2):
            out_ref[pl.ds((b // 5) * 32, 32), pl.ds((5 * h + b % 5) * 128, 128)] = total[
                h * 32 : (h + 1) * 32
            ]


def inverse_kernel(in_ref, scatter_ref, twiddle_ref, table_ref, out_ref, c_ref, z_ref):
    for part in range(4):
        for i in range(5):
            c_ref[part, i, pl.ds(56, 8), :] = jnp.zeros((8, LANES), F32)
    for u in range(10):
        high, low = split(in_ref[:, pl.ds(u * 128, 128)])
        moved = dot_t(scatter_ref[...], high) + dot_t(scatter_ref[...], low)
        for part in range(4):
            for i in range(5):
                start = (part * 5 + i) * 8
                c_ref[part, i, pl.ds(u, 6, stride=10), :] = moved[start : start + 6]
    table_hi = table_ref[pl.ds(0, 512), :]
    table_lo = table_ref[pl.ds(512, 512), :]
    lane_owner = (lax.broadcasted_iota(jnp.int32, (64, 512), 1) % 128) // 32
    for i in range(5):
        block = jnp.concatenate([c_ref[part, i] for part in range(4)], axis=1)
        for b1 in range(4):
            high, low = split(jnp.where(lane_owner == b1, block, 0.0))
            first = dot(jnp.concatenate([high, low], axis=0), table_hi)
            z_ref[5 * b1 + i] = first[:64] + first[64:] + dot(high, table_lo)

    @pl.loop(0, 8)
    def _(group):
        rows = pl.ds(pl.multiple_of(group * 8, 8), 8)
        z = {}
        for b in range(20):
            zr = z_ref[b, rows, pl.ds(0, 128)]
            zi = z_ref[b, rows, pl.ds(128, 128)]
            tr = twiddle_ref[pl.ds(2 * b, 1), :]
            ti = twiddle_ref[pl.ds(2 * b + 1, 1), :]
            z[b % 4, b % 5] = (zr * tr - zi * ti, zr * ti + zi * tr)
        parts = [[None] * 5 for _ in range(4)]
        for b5 in range(5):
            r0, i0 = z[0, b5]
            r1, i1 = z[1, b5]
            r2, i2 = z[2, b5]
            r3, i3 = z[3, b5]
            er, ei, dr, di = r0 + r2, i0 + i2, r0 - r2, i0 - i2
            sr, si, fr, fi = r1 + r3, i1 + i3, r1 - r3, i1 - i3
            parts[0][b5] = (er + sr, ei + si)
            parts[2][b5] = (er - sr, ei - si)
            parts[1][b5] = (dr - fi, di + fr)
            parts[3][b5] = (dr + fi, di - fr)
        for n4 in range(4):
            t = parts[n4]
            base = t[0][0]
            p1, p2 = t[1][0] + t[4][0], t[2][0] + t[3][0]
            q1, q2 = t[1][1] - t[4][1], t[2][1] - t[3][1]
            m1, m2 = base + C1 * p1 + C2 * p2, base + C2 * p1 + C1 * p2
            n1, n2 = S1 * q1 + S2 * q2, S2 * q1 - S1 * q2
            for n5, value in enumerate((base + p1 + p2, m1 - n1, m2 - n2, m2 + n2, m1 + n1)):
                i2 = (4 * n5 + 5 * n4) % 20
                out_ref[i2 // 5, rows, pl.ds((i2 % 5) * 128, 128)] = value


def legendre_kernel(
    rank_ref,
    logs_ref,
    geo_ref,
    in_ref,
    lat_ref,
    gather_ref,
    fold_ref,
    unfold_ref,
    out_ref,
    a_ref,
    x_ref,
    coef_ref,
    state_ref,
    reset_ref,
    even_ref,
    odd_ref,
    acc_ref,
):
    rank = rank_ref[0]
    first = (rank % 32) * 20 + (rank // 32) * 5
    sub = lax.broadcasted_iota(jnp.int32, (8, LANES), 0)
    lane = lax.broadcasted_iota(jnp.int32, (8, LANES), 1)

    for u in range(10):
        a_ref[u, pl.ds(120, 8), :] = jnp.zeros((8, LANES), F32)
    for pair in range(5):
        high, low = split(in_ref[:, pl.ds(pair * 256, 256)])
        moved = dot_t(gather_ref[...], high) + dot_t(gather_ref[...], low)
        for u in range(10):
            for f in range(3):
                start = (u * 3 + f) * 8
                a_ref[u, pl.ds(f * 40 + pair * 8, 8), :] = moved[start : start + 8]

    for v in range(TILES):
        lanes = pl.ds(v * LANES, LANES)
        joined = jnp.concatenate(
            [a_ref[2 * v], a_ref[2 * v + 1], a_ref[9 - 2 * v], a_ref[8 - 2 * v]], axis=1
        )
        high, low = split(joined)
        folded = dot(high, fold_ref[...]) + dot(low, fold_ref[...])
        cut = lat_ref[pl.ds(3, 1), lanes]
        weight = lat_ref[pl.ds(4, 1), lanes]
        factors = []
        for pair in range(5):
            q = 2 * pair + sub // 4
            wave = first + q + jnp.where(q >= 5, 635, 0)
            excess = jnp.maximum(wave.astype(F32) - cut, 0.0) / filter_width
            doubling = jnp.where(wave == 0, 1.0, 2.0)
            factors.append(weight * jnp.exp(-0.5 * excess * excess) * doubling)
        factors = jnp.concatenate(factors * 3 + [jnp.zeros((8, LANES), F32)], axis=0)
        for parity in range(2):
            high, low = split(folded[:, parity * LANES : (parity + 1) * LANES] * factors)
            x_ref[parity, pl.ds(0, 128), lanes] = high
            x_ref[parity, pl.ds(128, 128), lanes] = low

    for phase in range(2):
        shift = jnp.where(sub >= 5, 635 + 3 * phase, 0)
        wave = (first + sub + shift).astype(F32)
        logs = jnp.zeros((8, LANES), F32)
        for slot in range(8):
            offset = slot + (635 + 3 * phase if slot >= 5 else 0)
            offset = min(offset, 644)
            logs = jnp.where(sub == slot, logs_ref[first + offset], logs)
        for v in range(TILES):
            lanes = pl.ds(v * LANES, LANES)
            main = wave * lat_ref[pl.ds(1, 1), lanes]
            rest = wave * lat_ref[pl.ds(2, 1), lanes] + logs
            exponent = jnp.floor(main + rest)
            reset_ref[phase, 0, :, lanes] = -jnp.exp2((main - exponent) + rest)
            reset_ref[phase, 1, :, lanes] = exponent

    def coefficients(block, _):
        step = block * STEPS + lane
        late = (sub >= 5) & (block >= CHUNKS // 2)
        wave_now = first + sub + jnp.where(sub >= 5, 635, 0) + jnp.where(late, 3, 0)
        excess = step - jnp.where(late, MMAX // 2, 0)
        live = (wave_now + excess < MMAX) & (jnp.logical_not(late) | (sub < 7))
        wave = wave_now.astype(F32)
        k = excess.astype(F32)
        degree = wave + k
        growth = jnp.sqrt((4.0 * degree * degree - 1.0) / jnp.maximum(k * (2.0 * wave + k), 1.0))
        backward = jnp.sqrt(
            jnp.maximum((k - 1.0) * (2.0 * wave + k - 1.0), 0.0)
            / jnp.maximum(4.0 * (degree - 1.0) * (degree - 1.0) - 1.0, 1.0)
        )
        start = excess == 0
        coef_ref[block, 0] = jnp.where(live & jnp.logical_not(start), growth, 0.0)
        coef_ref[block, 1] = jnp.where(live, jnp.where(start, 1.0, growth * backward), 0.0)
        return 0

    lax.fori_loop(0, CHUNKS + 1, coefficients, 0)
    for v in range(TILES):
        lanes = pl.ds(v * LANES, LANES)
        state_ref[0, :, lanes] = jnp.zeros((8, LANES), F32)
        state_ref[1, :, lanes] = reset_ref[0, 0, :, lanes]
        state_ref[2, :, lanes] = reset_ref[0, 1, :, lanes]
    acc_ref[...] = jnp.zeros_like(acc_ref)

    def generate(block, buf_ref):
        swap = (sub >= 5) & (block == CHUNKS // 2)
        newer, older, power, scale, cosine = [], [], [], [], []
        for v in range(TILES):
            lanes = pl.ds(v * LANES, LANES)
            newer.append(jnp.where(swap, 0.0, state_ref[0, :, lanes]))
            older.append(jnp.where(swap, reset_ref[1, 0, :, lanes], state_ref[1, :, lanes]))
            power.append(jnp.where(swap, reset_ref[1, 1, :, lanes], state_ref[2, :, lanes]))
            cosine.append(jnp.broadcast_to(lat_ref[pl.ds(0, 1), lanes], (8, LANES)))
            scale.append(jnp.where(power[v] < -126.0, 0.0, jnp.exp2(power[v])))
        growth = coef_ref[block, 0]
        backward = coef_ref[block, 1]
        held = {}
        for t in range(STEPS):
            a = jnp.broadcast_to(growth[:, t : t + 1], (8, LANES))
            c = jnp.broadcast_to(backward[:, t : t + 1], (8, LANES))
            for v in range(TILES):
                value = (a * cosine[v]) * newer[v] - c * older[v]
                older[v], newer[v] = newer[v], value
                held[t, v] = value * scale[v]
            if t % 8 == 7:
                for v in range(TILES):
                    large = jnp.abs(newer[v]) > renorm_big
                    factor = jnp.where(large, 1.0 / renorm_big, 1.0)
                    newer[v] = newer[v] * factor
                    older[v] = older[v] * factor
                    power[v] = power[v] + jnp.where(large, renorm_step, 0.0)
                    scale[v] = jnp.where(power[v] < -126.0, 0.0, jnp.exp2(power[v]))
            if t % 4 == 3:
                rows = pl.ds((t // 4) * 16, 16)
                for v in range(TILES):
                    lanes = pl.ds(v * LANES, LANES)
                    for parity in range(2):
                        both = jnp.concatenate(
                            [held.pop((t - 3 + parity, v)), held.pop((t - 1 + parity, v))], axis=0
                        )
                        high, low = split(both)
                        buf_ref[parity, 0, rows, lanes] = high
                        buf_ref[parity, 1, rows, lanes] = low
        for v in range(TILES):
            lanes = pl.ds(v * LANES, LANES)
            state_ref[0, :, lanes] = newer[v]
            state_ref[1, :, lanes] = older[v]
            state_ref[2, :, lanes] = power[v]

    geopot = jnp.where(sub % 2 == 0, geo_ref[0], geo_ref[1])

    def apply(block, buf_ref):
        late = block >= CHUNKS // 2
        slot = lane % 8
        upper = slot >= 5
        wave = first + slot + jnp.where(upper, jnp.where(late, 638 - MMAX // 2, 635), 0)
        owner = slot + jnp.where(upper & late, 3, 0)
        for parity in range(2):
            table_hi = buf_ref[parity, 0]
            table_lo = buf_ref[parity, 1]
            both = dot_t(x_ref[parity], table_hi)
            spectral = both[:128] + both[128:] + dot_t(x_ref[parity, pl.ds(0, 128), :], table_lo)
            halves = []
            for half in range(2):
                step = block * STEPS + 2 * (half * 16 + lane // 8) + parity
                degree = (wave + step).astype(F32)
                ratio = degree * (degree + 1.0) * (1.0 / (MMAX * MMAX))
                coupling = jnp.sqrt(ratio)
                damping = 1.0 / (1.0 + diffusion * ratio * ratio)
                shared = damping / (1.0 + geopot * ratio)
                cross = geopot * coupling
                vort, div, height = [], [], []
                for pair in range(5):
                    mine = owner == 2 * pair + sub // 4
                    part = spectral[:, half * LANES : (half + 1) * LANES]
                    v_part = part[pair * 8 : pair * 8 + 8]
                    d_part = part[40 + pair * 8 : 48 + pair * 8]
                    h_part = part[80 + pair * 8 : 88 + pair * 8]
                    mixed = jnp.where(mine, shared, 0.0)
                    vort.append(jnp.where(mine, damping, 0.0) * v_part)
                    div.append(mixed * (d_part + coupling * h_part))
                    height.append(mixed * (h_part - cross * d_part))
                halves.append(
                    jnp.concatenate(vort + div + height + [jnp.zeros((8, LANES), F32)], axis=0)
                )
            high, low = split(jnp.concatenate(halves, axis=1))
            both = dot(jnp.concatenate([high, low], axis=0), table_hi)
            acc_ref[parity] += both[:128] + both[128:] + dot(high, table_lo)

    generate(0, even_ref)

    @pl.loop(0, CHUNKS // 2)
    def _(pair):
        generate(2 * pair + 1, odd_ref)
        apply(2 * pair, even_ref)
        generate(2 * pair + 2, even_ref)
        apply(2 * pair + 1, odd_ref)

    for v in range(TILES):
        lanes = pl.ds(v * LANES, LANES)
        joined = jnp.concatenate([acc_ref[0, :, lanes], acc_ref[1, :, lanes]], axis=1)
        high, low = split(joined)
        moved = dot_t(unfold_ref[...], high) + dot_t(unfold_ref[...], low)
        for part, u in enumerate((2 * v, 2 * v + 1, 9 - 2 * v, 8 - 2 * v)):
            out_ref[pl.ds((part // 2) * 64, 64), pl.ds(u * LANES, LANES)] = moved[
                part * 64 : part * 64 + 64
            ]


VMEM = pl.BlockSpec(memory_space=pltpu.VMEM)
SMEM = pl.BlockSpec(memory_space=pltpu.SMEM)


def call(kernel, outputs, specs, scratch, megabytes, flops, name):
    shapes = tuple(jax.ShapeDtypeStruct(shape, F32) for shape in outputs)
    single = len(shapes) == 1
    return pl.pallas_call(
        kernel,
        out_shape=shapes[0] if single else shapes,
        in_specs=specs,
        out_specs=VMEM if single else tuple(VMEM for _ in shapes),
        scratch_shapes=scratch,
        compiler_params=pltpu.CompilerParams(vmem_limit_bytes=megabytes << 20),
        cost_estimate=pl.CostEstimate(flops=flops, bytes_accessed=2 << 20, transcendentals=0),
        name=name,
    )


def shards(vorticity, divergence, height, mean_geopot):
    rank = lax.axis_index("lat") * lax.axis_size("lon") + lax.axis_index("lon")
    rank = rank.astype(jnp.int32).reshape(1)
    twiddle = jnp.asarray(twiddles())
    packed = call(pack_kernel, [(4, 64, 640)], [VMEM] * 3, [], 8, 1 << 20, "pack")(
        vorticity, divergence, height
    )
    sectors = lax.all_to_all(packed, "lon", split_axis=0, concat_axis=0, tiled=True)
    spectrum = call(
        forward_kernel,
        [(128, 1280)],
        [VMEM] * 3,
        [pltpu.VMEM((20, 64, 256), F32)],
        16,
        1 << 28,
        "forward",
    )(sectors, twiddle, jnp.asarray(forward_matrix()))
    columns = lax.all_to_all(spectrum, ("lat", "lon"), split_axis=0, concat_axis=0, tiled=True)
    synthesis = call(
        legendre_kernel,
        [(128, 1280)],
        [SMEM] * 3 + [VMEM] * 5,
        [
            pltpu.VMEM((10, 128, LANES), F32),
            pltpu.VMEM((2, 256, 640), BF16),
            pltpu.VMEM((CHUNKS + 1, 2, 8, LANES), F32),
            pltpu.VMEM((3, 8, 640), F32),
            pltpu.VMEM((2, 2, 8, 640), F32),
            pltpu.VMEM((2, 2, 256, 640), BF16),
            pltpu.VMEM((2, 2, 256, 640), BF16),
            pltpu.VMEM((2, 128, 640), F32),
        ],
        32,
        1 << 33,
        "legendre",
    )(
        rank,
        jnp.asarray(sector_logs()),
        mean_geopot,
        columns,
        jnp.asarray(latitude_rows()),
        jnp.asarray(gather_matrix()),
        jnp.asarray(fold_matrix()),
        jnp.asarray(unfold_matrix()),
    )
    gathered = lax.all_to_all(synthesis, ("lat", "lon"), split_axis=0, concat_axis=0, tiled=True)
    result = call(
        inverse_kernel,
        [(4, 64, 640)],
        [VMEM] * 4,
        [pltpu.VMEM((4, 5, 64, LANES), F32), pltpu.VMEM((20, 64, 256), F32)],
        16,
        1 << 28,
        "inverse",
    )(gathered, jnp.asarray(scatter_matrix()), twiddle, jnp.asarray(inverse_matrix()))
    pieces = lax.all_to_all(result, "lon", split_axis=0, concat_axis=0, tiled=True)
    return call(unpack_kernel, [(2, 40, 640)] * 3, [VMEM], [], 8, 1 << 20, "unpack")(pieces)


def solution(mesh):
    placed = (P(None, "lat", "lon"), P(None, "lat", "lon"), P(None, "lat", "lon"), P())
    return jax.shard_map(
        shards,
        mesh=mesh,
        in_specs=placed,
        out_specs=(P(None, "lat", "lon"), P(None, "lat", "lon"), P(None, "lat", "lon")),
        check_vma=False,
    )
```

time: 1670 us -> 127 us (0.08)
  other arithmetic: 1100 us -> 0 us
  local copies, waits for them, and re-layouts: 332 us -> 6.72 us
  matrix products: 141 us -> 0 us
  Pallas kernels: 0 us -> 45.7 us
  starting transfers between devices: 39.6 us -> 8.01 us
  blocking collectives: 24.6 us -> 50.6 us
  loops' own time: 20 us -> 0 us
    while x1260 -> x0, other arithmetic: 965 us -> none
    dot_general x4 -> x0, matrix products: 141 us -> none  [the longest x1 58.3 us: shards(): lax.dot_general(columns, legendre, (((2,), (2,)), ((0,), (0,))), precisio...]
    dynamic_update_slice x20 -> x0, local copies, waits for them, and re-layouts: 123 us -> none  [block_step(): lax.dynamic_update_slice(table_now, jnp.stack(row_list, axis=1), (anchor,...]
    neg x1 -> x0, other arithmetic: 54.7 us -> none  [fourier_table(): -jnp.sin(phase_angle)]
    unnamed x26 -> x28, local copies, waits for them, and re-layouts: 56.7 us -> 4.51 us
    reshape x8 -> x0, local copies, waits for them, and re-layouts: 47.8 us -> none  [the longest x1 31.5 us: fourier_table(): jnp.stack([jnp.cos(phase_angle), -jnp.sin(phase_angle)], axis=-1)]
    pallas_call x0 -> x5, Pallas kernels: none -> 45.7 us  [the longest x1 40.6 us: shards(): call(legendre_kernel, [(128, 1280)], [SMEM] * 3 + [VMEM] * 5, [pltpu.VMEM...]
    another operation x8 -> x0, local copies, waits for them, and re-layouts: 39.4 us -> none  [the longest x1 38.9 us: fourier_table(): jnp.stack([jnp.cos(phase_angle), -jnp.sin(phase_angle)], axis=-1)]
  transfers between devices with their start and end apart: 7 -> 1, of which waited for: 1 -> 1; matrix products, arithmetic and copies ran while one was open for 81% -> 0% of each run, Pallas kernels for 0% -> 0%
where the time goes in v1:
time: 127 us; the launch traced here: 126 us
  blocking collectives  50.6 us (40%)
  Pallas kernels  45.7 us (36%)
  waiting for transfers between devices  14.6 us (11%)
  starting transfers between devices  8.01 us (6%)
  local copies, waits for them, and re-layouts  6.72 us (5%)
    pallas_call x1, Pallas kernels, shards(): call(legendre_kernel, [(128, 1280)], [SMEM] * 3 + [VMEM] * 5, [pltpu.VMEM...  40.6 us
    all_to_all x1, blocking collectives, shards(): lax.all_to_all(synthesis, ('lat', 'lon'), split_axis=0, concat_axis=0, ti...  19.2 us
    all_to_all x1, blocking collectives, shards(): lax.all_to_all(packed, 'lon', split_axis=0, concat_axis=0, tiled=True)  17.3 us
    all_to_all x1, waiting for transfers between devices, shards(): lax.all_to_all(spectrum, ('lat', 'lon'), split_axis=0, concat_axis=0, til...  14.6 us
    all_to_all x1, blocking collectives, shards(): lax.all_to_all(result, 'lon', split_axis=0, concat_axis=0, tiled=True)  14 us
    all_to_all x1, starting transfers between devices, shards(): lax.all_to_all(spectrum, ('lat', 'lon'), split_axis=0, concat_axis=0, til...  8.01 us
    unnamed x28, local copies, waits for them, and re-layouts  4.51 us
    pallas_call x1, Pallas kernels, shards(): call(inverse_kernel, [(4, 64, 640)], [VMEM] * 4, [pltpu.VMEM((4, 5, 64, L...  2.8 us
  transfers between devices with their start and end apart: 1, of which 1 were waited for; matrix products, arithmetic and copies ran while one was open for 0% of the time, Pallas kernels for 0%

profile of v1, /device:TPU:1, one launch (start us, length us, event | category | flops | bytes accessed | tf_op | source)
XLA Modules:
  0.0 126.4 jit_solution(8701516491167751485)
XLA Ops:
  0.6 0.0 copy-start.1
  0.6 0.9 copy-done.1
  1.6 0.0 copy-start.2
  1.6 0.9 copy-done.2
  2.5 0.0 copy-start.3
  2.5 0.9 copy-done.3
  3.4 0.1 pack.1
  3.5 0.0 copy-start.4
  3.5 0.0 copy-start.5
  3.5 17.3 %all_to_all.32.in_ref = f32[4,64,640]{2,1,0:T(8,128)S(1)} all-to-all(f32[4,64,640]{2,1,0:T(8,128)S(1)} %pack.1), channel_id=1, replica_groups=mesh['lat'=32,'lon'=4] {'lon'}, dimensions={0} | all-to-all | bytes 1310720 | tf_op jit(solution)/shard_map/all_to_all | solution.py:511
  20.8 0.0 copy-done.4
  20.8 0.0 copy-done.5
  20.9 1.3 %forward.1 = f32[128,1280]{1,0:T(8,128)S(1)} custom-call(f32[4,64,640]{2,1,0:T(8,128)S(1)} %all_to_all.32.in_ref, f32[40,128]{1,0:T(8,128)S(1)} %copy-done.4, bf16[128,256]{1,0:T(8,128)(2,1)S(1)} %copy-done.5), custom_call_target="tpu_custom_call" | custom-call | flops 268435456 | bytes 2097152 | tf_op jit(solution)/shard_map/forward/pallas_call | solution.py:512
  22.1 1.5 %copy.16 = f32[128,1,1280]{2,1,0:T(1,128)} copy(f32[128,1,1280]{2,0,1:T(8,128)S(1)} %bitcast.9) | data formatting | bytes 1310720 | tf_op jit(solution)/shard_map/all_to_all | solution.py:521
  23.7 8.0 %all-to-all-start.1 = ((f32[128,1,1280]{2,1,0:T(1,128)}), f32[128,1,1280]{2,1,0:T(1,128)S(1)}, u32[]{:S(2)}, u32[]{:S(2)}) async-start(f32[128,1,1280]{2,1,0:T(1,128)} %copy.16), calls=%async_computation.1 | async-start | bytes 1310720 | tf_op jit(solution)/shard_map/all_to_all | solution.py:521
  31.7 0.0 copy-start.8
  31.7 0.0 copy-start.9
  31.7 0.0 copy-start.10
  31.7 0.0 copy-start.11
  31.8 0.0 copy-start.12
  31.8 14.6 %all-to-all-done.1 = f32[128,1,1280]{2,1,0:T(1,128)S(1)} async-done(((f32[128,1,1280]{2,1,0:T(1,128)}), f32[128,1,1280]{2,1,0:T(1,128)S(1)}, u32[]{:S(2)}, u32[]{:S(2)}) %all-to-all-start.1) | async-done | bytes 655392 | tf_op jit(solution)/shard_map/all_to_all | solution.py:521
  46.5 0.0 copy-start.7
  46.5 0.0 copy-done.8
  46.5 0.0 copy-done.9
  46.5 0.0 copy-done.10
  46.5 0.0 copy-done.11
  46.5 0.0 copy-done.12
  46.5 0.6 copy-done.7
  47.1 40.6 %legendre.1 = f32[128,1280]{1,0:T(8,128)S(1)} custom-call(s32[1]{0:T(128)} %bitcast.rank_ref, f32[1280]{0:T(1024)S(1)} %copy-done.12, f32[2]{0:T(128)S(1)} %copy-done.7, f32[128,1280]{1,0:T(8,128)S(1)} %bitcast.11, f32[8,640]{1,0:T(8,128)S(1)} %copy-done.11, bf16[240,256]{1,0:T(8,128)(2,1)S(1)} %copy-done.10, bf16[512,256]{1,0:T(8,128)(2,1)S(1)} %copy-done.8, ...), custom_call_target="tpu_custom_call" | custom-call | flops 8589934592 | bytes 2097152 | tf_op jit(solution)/shard_map/legendre/pallas_call | solution.py:522
  87.7 0.7 copy.17
  88.4 19.2 %all_to_all.33 = f32[128,1,1280]{2,1,0:T(1,128)S(1)} all-to-all(f32[128,1,1280]{2,1,0:T(1,128)S(1)} %copy.17), channel_id=1, replica_groups=mesh['lat'=32,'lon'=4] {'lat','lon'}, dimensions={0} | all-to-all | bytes 1310720 | tf_op jit(solution)/shard_map/all_to_all | solution.py:549
  107.6 0.0 copy-start
  107.6 0.0 copy-start.6
  107.7 1.0 copy-done
  108.7 0.0 copy-done.6
  108.7 2.8 %inverse.1 = f32[4,64,640]{2,1,0:T(8,128)S(1)} custom-call(f32[128,1280]{1,0:T(8,128)S(1)} %bitcast.10, bf16[160,128]{1,0:T(8,128)(2,1)S(1)} %copy-done.6, f32[40,128]{1,0:T(8,128)S(1)} %copy-done.4, bf16[1024,256]{1,0:T(8,128)(2,1)S(1)} %copy-done), custom_call_target="tpu_custom_call" | custom-call | flops 268435456 | bytes 2097152 | tf_op jit(solution)/shard_map/inverse/pallas_call | solution.py:550
  111.5 14.0 %all_to_all.34.in_ref = f32[4,64,640]{2,1,0:T(8,128)S(1)} all-to-all(f32[4,64,640]{2,1,0:T(8,128)S(1)} %inverse.1), channel_id=1, replica_groups=mesh['lat'=32,'lon'=4] {'lon'}, dimensions={0} | all-to-all | bytes 1310720 | tf_op jit(solution)/shard_map/all_to_all | solution.py:559
  125.5 0.9 unpack.1
  (2 shorter events, 0.1 us)
Async XLA Ops:
  0.6 0.9 copy-start.1
  1.6 0.9 copy-start.2
  2.5 0.9 copy-start.3
  3.5 17.3 %copy-start.4 = (f32[40,128]{1,0:T(8,128)S(1)}, f32[40,128]{1,0:T(8,128)}, u32[]{:S(2)}) copy-start(f32[40,128]{1,0:T(8,128)} %constant.29.clone.twiddle_ref) | copy-start | bytes 61444
  3.5 17.3 %copy-start.5 = (bf16[128,256]{1,0:T(8,128)(2,1)S(1)}, bf16[128,256]{1,0:T(8,128)(2,1)}, u32[]{:S(2)}) copy-start(bf16[128,256]{1,0:T(8,128)(2,1)} %constant.30.clone.table_ref) | copy-start | bytes 196612
  23.7 22.7 %all-to-all-start.1 = ((f32[128,1,1280]{2,1,0:T(1,128)}), f32[128,1,1280]{2,1,0:T(1,128)S(1)}, u32[]{:S(2)}, u32[]{:S(2)}) async-start(f32[128,1,1280]{2,1,0:T(1,128)} %copy.16), calls=%async_computation.1 | async-start | bytes 1310720 | tf_op jit(solution)/shard_map/all_to_all | solution.py:521
  31.7 14.8 %copy-start.8 = (bf16[512,256]{1,0:T(8,128)(2,1)S(1)}, bf16[512,256]{1,0:T(8,128)(2,1)}, u32[]{:S(2)}) copy-start(bf16[512,256]{1,0:T(8,128)(2,1)} %constant.34.clone.fold_ref) | copy-start | bytes 786436
  31.7 14.8 %copy-start.9 = (bf16[256,256]{1,0:T(8,128)(2,1)S(1)}, bf16[256,256]{1,0:T(8,128)(2,1)}, u32[]{:S(2)}) copy-start(bf16[256,256]{1,0:T(8,128)(2,1)} %constant.35.clone.unfold_ref) | copy-start | bytes 393220
  31.7 14.8 %copy-start.10 = (bf16[240,256]{1,0:T(8,128)(2,1)S(1)}, bf16[240,256]{1,0:T(8,128)(2,1)}, u32[]{:S(2)}) copy-start(bf16[240,256]{1,0:T(8,128)(2,1)} %constant.33.clone.gather_ref) | copy-start | bytes 368644
  31.7 14.8 %copy-start.11 = (f32[8,640]{1,0:T(8,128)S(1)}, f32[8,640]{1,0:T(8,128)}, u32[]{:S(2)}) copy-start(f32[8,640]{1,0:T(8,128)} %constant.32.clone.lat_ref) | copy-start | bytes 61444
  31.8 14.8 %copy-start.12 = (f32[1280]{0:T(1024)S(1)}, f32[1280]{0:T(1024)}, u32[]{:S(2)}) copy-start(f32[1280]{0:T(1024)} %constant.31.clone.logs_ref) | copy-start | bytes 15364
  46.5 0.7 copy-start.7
  107.6 1.0 copy-start
  107.6 1.0 copy-start.6

commit v2 on v1

--- a/solution.py
+++ b/solution.py
@@ -293,8 +293,12 @@
     coef_ref,
     state_ref,
     reset_ref,
-    even_ref,
-    odd_ref,
+    table0_ref,
+    table1_ref,
+    table2_ref,
+    update0_ref,
+    update1_ref,
+    update2_ref,
     acc_ref,
 ):
     rank = rank_ref[0]
@@ -369,7 +373,7 @@
         coef_ref[block, 1] = jnp.where(live, jnp.where(start, 1.0, growth * backward), 0.0)
         return 0
 
-    lax.fori_loop(0, CHUNKS + 1, coefficients, 0)
+    lax.fori_loop(0, CHUNKS + 3, coefficients, 0)
     for v in range(TILES):
         lanes = pl.ds(v * LANES, LANES)
         state_ref[0, :, lanes] = jnp.zeros((8, LANES), F32)
@@ -424,52 +428,71 @@
 
     geopot = jnp.where(sub % 2 == 0, geo_ref[0], geo_ref[1])
 
-    def apply(block, buf_ref):
+    def analyse(block, parity, buf_ref, update_ref):
         late = block >= CHUNKS // 2
         slot = lane % 8
         upper = slot >= 5
         wave = first + slot + jnp.where(upper, jnp.where(late, 638 - MMAX // 2, 635), 0)
         owner = slot + jnp.where(upper & late, 3, 0)
-        for parity in range(2):
-            table_hi = buf_ref[parity, 0]
-            table_lo = buf_ref[parity, 1]
-            both = dot_t(x_ref[parity], table_hi)
-            spectral = both[:128] + both[128:] + dot_t(x_ref[parity, pl.ds(0, 128), :], table_lo)
-            halves = []
-            for half in range(2):
-                step = block * STEPS + 2 * (half * 16 + lane // 8) + parity
-                degree = (wave + step).astype(F32)
-                ratio = degree * (degree + 1.0) * (1.0 / (MMAX * MMAX))
-                coupling = jnp.sqrt(ratio)
-                damping = 1.0 / (1.0 + diffusion * ratio * ratio)
-                shared = damping / (1.0 + geopot * ratio)
-                cross = geopot * coupling
-                vort, div, height = [], [], []
-                for pair in range(5):
-                    mine = owner == 2 * pair + sub // 4
-                    part = spectral[:, half * LANES : (half + 1) * LANES]
-                    v_part = part[pair * 8 : pair * 8 + 8]
-                    d_part = part[40 + pair * 8 : 48 + pair * 8]
-                    h_part = part[80 + pair * 8 : 88 + pair * 8]
-                    mixed = jnp.where(mine, shared, 0.0)
-                    vort.append(jnp.where(mine, damping, 0.0) * v_part)
-                    div.append(mixed * (d_part + coupling * h_part))
-                    height.append(mixed * (h_part - cross * d_part))
-                halves.append(
-                    jnp.concatenate(vort + div + height + [jnp.zeros((8, LANES), F32)], axis=0)
-                )
-            high, low = split(jnp.concatenate(halves, axis=1))
-            both = dot(jnp.concatenate([high, low], axis=0), table_hi)
-            acc_ref[parity] += both[:128] + both[128:] + dot(high, table_lo)
-
-    generate(0, even_ref)
-
-    @pl.loop(0, CHUNKS // 2)
-    def _(pair):
-        generate(2 * pair + 1, odd_ref)
-        apply(2 * pair, even_ref)
-        generate(2 * pair + 2, even_ref)
-        apply(2 * pair + 1, odd_ref)
+        both = dot_t(x_ref[parity], buf_ref[parity, 0])
+        spectral = both[:128] + both[128:] + dot_t(
+            x_ref[parity, pl.ds(0, 128), :], buf_ref[parity, 1]
+        )
+        halves = []
+        for half in range(2):
+            step = block * STEPS + 2 * (half * 16 + lane // 8) + parity
+            degree = (wave + step).astype(F32)
+            ratio = degree * (degree + 1.0) * (1.0 / (MMAX * MMAX))
+            coupling = jnp.sqrt(ratio)
+            damping = 1.0 / (1.0 + diffusion * ratio * ratio)
+            shared = damping / (1.0 + geopot * ratio)
+            cross = geopot * coupling
+            part = spectral[:, half * LANES : (half + 1) * LANES]
+            vort, div, height = [], [], []
+            for pair in range(5):
+                mine = owner == 2 * pair + sub // 4
+                v_part = part[pair * 8 : pair * 8 + 8]
+                d_part = part[40 + pair * 8 : 48 + pair * 8]
+                h_part = part[80 + pair * 8 : 88 + pair * 8]
+                mixed = jnp.where(mine, shared, 0.0)
+                vort.append(jnp.where(mine, damping, 0.0) * v_part)
+                div.append(mixed * (d_part + coupling * h_part))
+                height.append(mixed * (h_part - cross * d_part))
+            halves.append(
+                jnp.concatenate(vort + div + height + [jnp.zeros((8, LANES), F32)], axis=0)
+            )
+        high, low = split(jnp.concatenate(halves, axis=1))
+        update_ref[parity, pl.ds(0, 128), :] = high
+        update_ref[parity, pl.ds(128, 128), :] = low
+
+    def synthesise(parity, buf_ref, update_ref):
+        both = dot(update_ref[parity], buf_ref[parity, 0])
+        rest = dot(update_ref[parity, pl.ds(0, 128), :], buf_ref[parity, 1])
+        acc_ref[parity] += both[:128] + both[128:] + rest
+
+    tables = (table0_ref, table1_ref, table2_ref)
+    updates = (update0_ref, update1_ref, update2_ref)
+    generate(0, tables[0])
+    generate(1, tables[1])
+    for parity in range(2):
+        analyse(0, parity, tables[0], updates[0])
+
+    @pl.loop(0, (CHUNKS + 2) // 3)
+    def _(group):
+        for turn in range(3):
+            block = 3 * group + turn
+
+            def advance(block=block, turn=turn):
+                now, later, last = turn, (turn + 1) % 3, (turn + 2) % 3
+                generate(block + 2, tables[last])
+                for parity in range(2):
+                    analyse(block + 1, parity, tables[later], updates[later])
+                    synthesise(parity, tables[now], updates[now])
+
+            if turn < 2:
+                advance()
+            else:
+                pl.when(block < CHUNKS)(advance)
 
     for v in range(TILES):
         lanes = pl.ds(v * LANES, LANES)
@@ -526,11 +549,11 @@
         [
             pltpu.VMEM((10, 128, LANES), F32),
             pltpu.VMEM((2, 256, 640), BF16),
-            pltpu.VMEM((CHUNKS + 1, 2, 8, LANES), F32),
+            pltpu.VMEM((CHUNKS + 3, 2, 8, LANES), F32),
             pltpu.VMEM((3, 8, 640), F32),
             pltpu.VMEM((2, 2, 8, 640), F32),
-            pltpu.VMEM((2, 2, 256, 640), BF16),
-            pltpu.VMEM((2, 2, 256, 640), BF16),
+            *[pltpu.VMEM((2, 2, 256, 640), BF16) for _ in range(3)],
+            *[pltpu.VMEM((2, 256, 256), BF16) for _ in range(3)],
             pltpu.VMEM((2, 128, 640), F32),
         ],
         32,

time: 127 us -> 112 us (0.88)
  Pallas kernels: 45.7 us -> 31.1 us
    pallas_call x1, Pallas kernels: 40.6 us -> 26 us  [shards(): call(legendre_kernel, [(128, 1280)], [SMEM] * 3 + [VMEM] * 5, [pltpu.VMEM...]
where the time goes in v2:
time: 112 us
  blocking collectives  50.6 us (45%)
  Pallas kernels  31.1 us (28%)
  waiting for transfers between devices  14.6 us (13%)
  starting transfers between devices  8.01 us (7%)
  local copies, waits for them, and re-layouts  6.72 us (6%)
    pallas_call x1, Pallas kernels, shards(): call(legendre_kernel, [(128, 1280)], [SMEM] * 3 + [VMEM] * 5, [pltpu.VMEM...  26 us
    all_to_all x1, blocking collectives, shards(): lax.all_to_all(synthesis, ('lat', 'lon'), split_axis=0, concat_axis=0, ti...  19.2 us
    all_to_all x1, blocking collectives, shards(): lax.all_to_all(packed, 'lon', split_axis=0, concat_axis=0, tiled=True)  17.3 us
    all_to_all x1, waiting for transfers between devices, shards(): lax.all_to_all(spectrum, ('lat', 'lon'), split_axis=0, concat_axis=0, til...  14.6 us
    all_to_all x1, blocking collectives, shards(): lax.all_to_all(result, 'lon', split_axis=0, concat_axis=0, tiled=True)  14 us
    all_to_all x1, starting transfers between devices, shards(): lax.all_to_all(spectrum, ('lat', 'lon'), split_axis=0, concat_axis=0, til...  8.01 us
    unnamed x28, local copies, waits for them, and re-layouts  4.51 us
    pallas_call x1, Pallas kernels, shards(): call(inverse_kernel, [(4, 64, 640)], [VMEM] * 4, [pltpu.VMEM((4, 5, 64, L...  2.81 us
  transfers between devices with their start and end apart: 1, of which 1 were waited for; matrix products, arithmetic and copies ran while one was open for 0% of the time, Pallas kernels for 0%

profile of v2, /device:TPU:1, one launch (start us, length us, event | category | flops | bytes accessed | tf_op | source)
XLA Modules:
  0.0 111.8 jit_solution(10772136083409414600)
XLA Ops:
  0.6 0.0 copy-start.1
  0.6 0.9 copy-done.1
  1.6 0.0 copy-start.2
  1.6 0.9 copy-done.2
  2.5 0.0 copy-start.3
  2.5 0.9 copy-done.3
  3.4 0.1 pack.1
  3.5 0.0 copy-start.4
  3.5 0.0 copy-start.5
  3.5 17.3 %all_to_all.32.in_ref = f32[4,64,640]{2,1,0:T(8,128)S(1)} all-to-all(f32[4,64,640]{2,1,0:T(8,128)S(1)} %pack.1), channel_id=1, replica_groups=mesh['lat'=32,'lon'=4] {'lon'}, dimensions={0} | all-to-all | bytes 1310720 | tf_op jit(solution)/shard_map/all_to_all | solution.py:534
  20.8 0.0 copy-done.4
  20.8 0.0 copy-done.5
  20.9 1.3 %forward.1 = f32[128,1280]{1,0:T(8,128)S(1)} custom-call(f32[4,64,640]{2,1,0:T(8,128)S(1)} %all_to_all.32.in_ref, f32[40,128]{1,0:T(8,128)S(1)} %copy-done.4, bf16[128,256]{1,0:T(8,128)(2,1)S(1)} %copy-done.5), custom_call_target="tpu_custom_call" | custom-call | flops 268435456 | bytes 2097152 | tf_op jit(solution)/shard_map/forward/pallas_call | solution.py:535
  22.1 1.5 %copy.16 = f32[128,1,1280]{2,1,0:T(1,128)} copy(f32[128,1,1280]{2,0,1:T(8,128)S(1)} %bitcast.9) | data formatting | bytes 1310720 | tf_op jit(solution)/shard_map/all_to_all | solution.py:544
  23.7 8.0 %all-to-all-start.1 = ((f32[128,1,1280]{2,1,0:T(1,128)}), f32[128,1,1280]{2,1,0:T(1,128)S(1)}, u32[]{:S(2)}, u32[]{:S(2)}) async-start(f32[128,1,1280]{2,1,0:T(1,128)} %copy.16), calls=%async_computation.1 | async-start | bytes 1310720 | tf_op jit(solution)/shard_map/all_to_all | solution.py:544
  31.7 0.0 copy-start.8
  31.7 0.0 copy-start.9
  31.7 0.0 copy-start.10
  31.7 0.0 copy-start.11
  31.8 0.0 copy-start.12
  31.8 14.6 %all-to-all-done.1 = f32[128,1,1280]{2,1,0:T(1,128)S(1)} async-done(((f32[128,1,1280]{2,1,0:T(1,128)}), f32[128,1,1280]{2,1,0:T(1,128)S(1)}, u32[]{:S(2)}, u32[]{:S(2)}) %all-to-all-start.1) | async-done | bytes 655392 | tf_op jit(solution)/shard_map/all_to_all | solution.py:544
  46.5 0.0 copy-start.7
  46.5 0.0 copy-done.8
  46.5 0.0 copy-done.9
  46.5 0.0 copy-done.10
  46.5 0.0 copy-done.11
  46.5 0.0 copy-done.12
  46.5 0.6 copy-done.7
  47.1 26.0 %legendre.1 = f32[128,1280]{1,0:T(8,128)S(1)} custom-call(s32[1]{0:T(128)} %bitcast.rank_ref, f32[1280]{0:T(1024)S(1)} %copy-done.12, f32[2]{0:T(128)S(1)} %copy-done.7, f32[128,1280]{1,0:T(8,128)S(1)} %bitcast.11, f32[8,640]{1,0:T(8,128)S(1)} %copy-done.11, bf16[240,256]{1,0:T(8,128)(2,1)S(1)} %copy-done.10, bf16[512,256]{1,0:T(8,128)(2,1)S(1)} %copy-done.8, ...), custom_call_target="tpu_custom_call" | custom-call | flops 8589934592 | bytes 2097152 | tf_op jit(solution)/shard_map/legendre/pallas_call | solution.py:545
  73.1 0.7 copy.17
  73.8 19.2 %all_to_all.33 = f32[128,1,1280]{2,1,0:T(1,128)S(1)} all-to-all(f32[128,1,1280]{2,1,0:T(1,128)S(1)} %copy.17), channel_id=1, replica_groups=mesh['lat'=32,'lon'=4] {'lat','lon'}, dimensions={0} | all-to-all | bytes 1310720 | tf_op jit(solution)/shard_map/all_to_all | solution.py:572
  93.0 0.0 copy-start
  93.0 0.0 copy-start.6
  93.1 1.0 copy-done
  94.1 0.0 copy-done.6
  94.1 2.8 %inverse.1 = f32[4,64,640]{2,1,0:T(8,128)S(1)} custom-call(f32[128,1280]{1,0:T(8,128)S(1)} %bitcast.10, bf16[160,128]{1,0:T(8,128)(2,1)S(1)} %copy-done.6, f32[40,128]{1,0:T(8,128)S(1)} %copy-done.4, bf16[1024,256]{1,0:T(8,128)(2,1)S(1)} %copy-done), custom_call_target="tpu_custom_call" | custom-call | flops 268435456 | bytes 2097152 | tf_op jit(solution)/shard_map/inverse/pallas_call | solution.py:573
  96.9 14.0 %all_to_all.34.in_ref = f32[4,64,640]{2,1,0:T(8,128)S(1)} all-to-all(f32[4,64,640]{2,1,0:T(8,128)S(1)} %inverse.1), channel_id=1, replica_groups=mesh['lat'=32,'lon'=4] {'lon'}, dimensions={0} | all-to-all | bytes 1310720 | tf_op jit(solution)/shard_map/all_to_all | solution.py:582
  110.9 0.9 unpack.1
  (2 shorter events, 0.1 us)
Async XLA Ops:
  0.6 0.9 copy-start.1
  1.6 0.9 copy-start.2
  2.5 0.9 copy-start.3
  3.5 17.3 %copy-start.4 = (f32[40,128]{1,0:T(8,128)S(1)}, f32[40,128]{1,0:T(8,128)}, u32[]{:S(2)}) copy-start(f32[40,128]{1,0:T(8,128)} %constant.29.clone.twiddle_ref) | copy-start | bytes 61444
  3.5 17.3 %copy-start.5 = (bf16[128,256]{1,0:T(8,128)(2,1)S(1)}, bf16[128,256]{1,0:T(8,128)(2,1)}, u32[]{:S(2)}) copy-start(bf16[128,256]{1,0:T(8,128)(2,1)} %constant.30.clone.table_ref) | copy-start | bytes 196612
  23.7 22.7 %all-to-all-start.1 = ((f32[128,1,1280]{2,1,0:T(1,128)}), f32[128,1,1280]{2,1,0:T(1,128)S(1)}, u32[]{:S(2)}, u32[]{:S(2)}) async-start(f32[128,1,1280]{2,1,0:T(1,128)} %copy.16), calls=%async_computation.1 | async-start | bytes 1310720 | tf_op jit(solution)/shard_map/all_to_all | solution.py:544
  31.7 14.8 %copy-start.8 = (bf16[512,256]{1,0:T(8,128)(2,1)S(1)}, bf16[512,256]{1,0:T(8,128)(2,1)}, u32[]{:S(2)}) copy-start(bf16[512,256]{1,0:T(8,128)(2,1)} %constant.34.clone.fold_ref) | copy-start | bytes 786436
  31.7 14.8 %copy-start.9 = (bf16[256,256]{1,0:T(8,128)(2,1)S(1)}, bf16[256,256]{1,0:T(8,128)(2,1)}, u32[]{:S(2)}) copy-start(bf16[256,256]{1,0:T(8,128)(2,1)} %constant.35.clone.unfold_ref) | copy-start | bytes 393220
  31.7 14.8 %copy-start.10 = (bf16[240,256]{1,0:T(8,128)(2,1)S(1)}, bf16[240,256]{1,0:T(8,128)(2,1)}, u32[]{:S(2)}) copy-start(bf16[240,256]{1,0:T(8,128)(2,1)} %constant.33.clone.gather_ref) | copy-start | bytes 368644
  31.7 14.8 %copy-start.11 = (f32[8,640]{1,0:T(8,128)S(1)}, f32[8,640]{1,0:T(8,128)}, u32[]{:S(2)}) copy-start(f32[8,640]{1,0:T(8,128)} %constant.32.clone.lat_ref) | copy-start | bytes 61444
  31.8 14.8 %copy-start.12 = (f32[1280]{0:T(1024)S(1)}, f32[1280]{0:T(1024)}, u32[]{:S(2)}) copy-start(f32[1280]{0:T(1024)} %constant.31.clone.logs_ref) | copy-start | bytes 15364
  46.5 0.7 copy-start.7
  93.0 1.0 copy-start
  93.0 1.0 copy-start.6

commit v3 on v2

--- a/solution.py
+++ b/solution.py
@@ -1,3 +1,5 @@
+import functools
+
 import jax
 import jax.numpy as jnp
 import ml_dtypes
@@ -14,6 +16,8 @@
 BF16 = jnp.bfloat16
 STEPS = 64
 CHUNKS = MMAX // STEPS
+HALF = CHUNKS // 2
+SLOTS = 4
 TILES = 5
 LANES = 128
 
@@ -143,12 +147,22 @@
 S1, S2 = float(np.sin(2 * np.pi / 5)), float(np.sin(4 * np.pi / 5))
 
 
-def pack_kernel(vort_ref, div_ref, height_ref, out_ref):
+def pack_kernel(vort_hbm, div_hbm, height_hbm, out_ref, vort_ref, div_ref, height_ref, sem_ref):
+    copies = [
+        pltpu.make_async_copy(source, target, sem_ref.at[index])
+        for index, (source, target) in enumerate(
+            ((vort_hbm, vort_ref), (div_hbm, div_ref), (height_hbm, height_ref))
+        )
+    ]
+    for copy in copies:
+        copy.start()
     for b in range(4):
-        for f, ref in enumerate((vort_ref, div_ref, height_ref)):
+        out_ref[b, pl.ds(60, 4), :] = jnp.zeros((4, 640), F32)
+    for f, ref in enumerate((vort_ref, div_ref, height_ref)):
+        copies[f].wait()
+        for b in range(4):
             for lev in range(2):
                 out_ref[b, pl.ds((2 * f + lev) * 10, 10), :] = ref[lev, pl.ds(10 * b, 10), :]
-        out_ref[b, pl.ds(60, 4), :] = jnp.zeros((4, 640), F32)
 
 
 def unpack_kernel(in_ref, vort_ref, div_ref, height_ref):
@@ -278,67 +292,17 @@
                 out_ref[i2 // 5, rows, pl.ds((i2 % 5) * 128, 128)] = value
 
 
-def legendre_kernel(
-    rank_ref,
-    logs_ref,
-    geo_ref,
-    in_ref,
-    lat_ref,
-    gather_ref,
-    fold_ref,
-    unfold_ref,
-    out_ref,
-    a_ref,
-    x_ref,
-    coef_ref,
-    state_ref,
-    reset_ref,
-    table0_ref,
-    table1_ref,
-    table2_ref,
-    update0_ref,
-    update1_ref,
-    update2_ref,
-    acc_ref,
-):
+def table_kernel(phase, rank_ref, logs_ref, lat_ref, before_ref, table_ref, state_ref, coef_ref):
     rank = rank_ref[0]
     first = (rank % 32) * 20 + (rank // 32) * 5
     sub = lax.broadcasted_iota(jnp.int32, (8, LANES), 0)
     lane = lax.broadcasted_iota(jnp.int32, (8, LANES), 1)
 
-    for u in range(10):
-        a_ref[u, pl.ds(120, 8), :] = jnp.zeros((8, LANES), F32)
-    for pair in range(5):
-        high, low = split(in_ref[:, pl.ds(pair * 256, 256)])
-        moved = dot_t(gather_ref[...], high) + dot_t(gather_ref[...], low)
-        for u in range(10):
-            for f in range(3):
-                start = (u * 3 + f) * 8
-                a_ref[u, pl.ds(f * 40 + pair * 8, 8), :] = moved[start : start + 8]
-
-    for v in range(TILES):
-        lanes = pl.ds(v * LANES, LANES)
-        joined = jnp.concatenate(
-            [a_ref[2 * v], a_ref[2 * v + 1], a_ref[9 - 2 * v], a_ref[8 - 2 * v]], axis=1
-        )
-        high, low = split(joined)
-        folded = dot(high, fold_ref[...]) + dot(low, fold_ref[...])
-        cut = lat_ref[pl.ds(3, 1), lanes]
-        weight = lat_ref[pl.ds(4, 1), lanes]
-        factors = []
-        for pair in range(5):
-            q = 2 * pair + sub // 4
-            wave = first + q + jnp.where(q >= 5, 635, 0)
-            excess = jnp.maximum(wave.astype(F32) - cut, 0.0) / filter_width
-            doubling = jnp.where(wave == 0, 1.0, 2.0)
-            factors.append(weight * jnp.exp(-0.5 * excess * excess) * doubling)
-        factors = jnp.concatenate(factors * 3 + [jnp.zeros((8, LANES), F32)], axis=0)
-        for parity in range(2):
-            high, low = split(folded[:, parity * LANES : (parity + 1) * LANES] * factors)
-            x_ref[parity, pl.ds(0, 128), lanes] = high
-            x_ref[parity, pl.ds(128, 128), lanes] = low
-
-    for phase in range(2):
+    step_index = pl.program_id(0)
+
+    @pl.when(step_index == 0)
+    def _():
+        fresh = (sub >= 5) | (phase == 0)
         shift = jnp.where(sub >= 5, 635 + 3 * phase, 0)
         wave = (first + sub + shift).astype(F32)
         logs = jnp.zeros((8, LANES), F32)
@@ -351,48 +315,44 @@
             main = wave * lat_ref[pl.ds(1, 1), lanes]
             rest = wave * lat_ref[pl.ds(2, 1), lanes] + logs
             exponent = jnp.floor(main + rest)
-            reset_ref[phase, 0, :, lanes] = -jnp.exp2((main - exponent) + rest)
-            reset_ref[phase, 1, :, lanes] = exponent
-
-    def coefficients(block, _):
-        step = block * STEPS + lane
-        late = (sub >= 5) & (block >= CHUNKS // 2)
-        wave_now = first + sub + jnp.where(sub >= 5, 635, 0) + jnp.where(late, 3, 0)
-        excess = step - jnp.where(late, MMAX // 2, 0)
-        live = (wave_now + excess < MMAX) & (jnp.logical_not(late) | (sub < 7))
-        wave = wave_now.astype(F32)
-        k = excess.astype(F32)
-        degree = wave + k
-        growth = jnp.sqrt((4.0 * degree * degree - 1.0) / jnp.maximum(k * (2.0 * wave + k), 1.0))
-        backward = jnp.sqrt(
-            jnp.maximum((k - 1.0) * (2.0 * wave + k - 1.0), 0.0)
-            / jnp.maximum(4.0 * (degree - 1.0) * (degree - 1.0) - 1.0, 1.0)
-        )
-        start = excess == 0
-        coef_ref[block, 0] = jnp.where(live & jnp.logical_not(start), growth, 0.0)
-        coef_ref[block, 1] = jnp.where(live, jnp.where(start, 1.0, growth * backward), 0.0)
-        return 0
-
-    lax.fori_loop(0, CHUNKS + 3, coefficients, 0)
-    for v in range(TILES):
-        lanes = pl.ds(v * LANES, LANES)
-        state_ref[0, :, lanes] = jnp.zeros((8, LANES), F32)
-        state_ref[1, :, lanes] = reset_ref[0, 0, :, lanes]
-        state_ref[2, :, lanes] = reset_ref[0, 1, :, lanes]
-    acc_ref[...] = jnp.zeros_like(acc_ref)
-
-    def generate(block, buf_ref):
-        swap = (sub >= 5) & (block == CHUNKS // 2)
+            start = -jnp.exp2((main - exponent) + rest)
+            state_ref[0, :, lanes] = jnp.where(fresh, 0.0, before_ref[0, :, lanes])
+            state_ref[1, :, lanes] = jnp.where(fresh, start, before_ref[1, :, lanes])
+            state_ref[2, :, lanes] = jnp.where(fresh, exponent, before_ref[2, :, lanes])
+
+        def coefficients(turn, _):
+            block = HALF * phase + turn
+            step = block * STEPS + lane
+            late = (sub >= 5) & (block >= CHUNKS // 2)
+            wave_now = first + sub + jnp.where(sub >= 5, 635, 0) + jnp.where(late, 3, 0)
+            excess = step - jnp.where(late, MMAX // 2, 0)
+            live = (wave_now + excess < MMAX) & (jnp.logical_not(late) | (sub < 7))
+            wave = wave_now.astype(F32)
+            k = excess.astype(F32)
+            degree = wave + k
+            growth = jnp.sqrt((4.0 * degree * degree - 1.0) / jnp.maximum(k * (2.0 * wave + k), 1.0))
+            backward = jnp.sqrt(
+                jnp.maximum((k - 1.0) * (2.0 * wave + k - 1.0), 0.0)
+                / jnp.maximum(4.0 * (degree - 1.0) * (degree - 1.0) - 1.0, 1.0)
+            )
+            start = excess == 0
+            coef_ref[turn, 0] = jnp.where(live & jnp.logical_not(start), growth, 0.0)
+            coef_ref[turn, 1] = jnp.where(live, jnp.where(start, 1.0, growth * backward), 0.0)
+            return 0
+
+        lax.fori_loop(0, HALF, coefficients, 0)
+
+    def generate():
         newer, older, power, scale, cosine = [], [], [], [], []
         for v in range(TILES):
             lanes = pl.ds(v * LANES, LANES)
-            newer.append(jnp.where(swap, 0.0, state_ref[0, :, lanes]))
-            older.append(jnp.where(swap, reset_ref[1, 0, :, lanes], state_ref[1, :, lanes]))
-            power.append(jnp.where(swap, reset_ref[1, 1, :, lanes], state_ref[2, :, lanes]))
+            newer.append(state_ref[0, :, lanes])
+            older.append(state_ref[1, :, lanes])
+            power.append(state_ref[2, :, lanes])
             cosine.append(jnp.broadcast_to(lat_ref[pl.ds(0, 1), lanes], (8, LANES)))
             scale.append(jnp.where(power[v] < -126.0, 0.0, jnp.exp2(power[v])))
-        growth = coef_ref[block, 0]
-        backward = coef_ref[block, 1]
+        growth = coef_ref[step_index, 0]
+        backward = coef_ref[step_index, 1]
         held = {}
         for t in range(STEPS):
             a = jnp.broadcast_to(growth[:, t : t + 1], (8, LANES))
@@ -418,25 +378,105 @@
                             [held.pop((t - 3 + parity, v)), held.pop((t - 1 + parity, v))], axis=0
                         )
                         high, low = split(both)
-                        buf_ref[parity, 0, rows, lanes] = high
-                        buf_ref[parity, 1, rows, lanes] = low
+                        table_ref[0, parity, 0, rows, lanes] = high
+                        table_ref[0, parity, 1, rows, lanes] = low
         for v in range(TILES):
             lanes = pl.ds(v * LANES, LANES)
             state_ref[0, :, lanes] = newer[v]
             state_ref[1, :, lanes] = older[v]
             state_ref[2, :, lanes] = power[v]
 
+    generate()
+
+
+def legendre_kernel(
+    rank_ref,
+    geo_ref,
+    in_ref,
+    lat_ref,
+    gather_ref,
+    fold_ref,
+    unfold_ref,
+    early_ref,
+    late_ref,
+    out_ref,
+    a_ref,
+    x_ref,
+    update0_ref,
+    update1_ref,
+    acc_ref,
+    table_ref,
+    sem_ref,
+):
+    rank = rank_ref[0]
+    first = (rank % 32) * 20 + (rank // 32) * 5
+    sub = lax.broadcasted_iota(jnp.int32, (8, LANES), 0)
+    lane = lax.broadcasted_iota(jnp.int32, (8, LANES), 1)
+
+    def fetch(block):
+        slot = block % SLOTS
+
+        @pl.when(block < HALF)
+        def _():
+            pltpu.make_async_copy(early_ref.at[block], table_ref.at[slot], sem_ref.at[slot]).start()
+
+        @pl.when((block >= HALF) & (block < CHUNKS))
+        def _():
+            pltpu.make_async_copy(
+                late_ref.at[block - HALF], table_ref.at[slot], sem_ref.at[slot]
+            ).start()
+
+    def arrived(block):
+        slot = block % SLOTS
+        pltpu.make_async_copy(early_ref.at[0], table_ref.at[slot], sem_ref.at[slot]).wait()
+
+    for block in range(3):
+        fetch(block)
+
+    for u in range(10):
+        a_ref[u, pl.ds(120, 8), :] = jnp.zeros((8, LANES), F32)
+    for pair in range(5):
+        high, low = split(in_ref[:, pl.ds(pair * 256, 256)])
+        moved = dot_t(gather_ref[...], high) + dot_t(gather_ref[...], low)
+        for u in range(10):
+            for f in range(3):
+                start = (u * 3 + f) * 8
+                a_ref[u, pl.ds(f * 40 + pair * 8, 8), :] = moved[start : start + 8]
+
+    for v in range(TILES):
+        lanes = pl.ds(v * LANES, LANES)
+        joined = jnp.concatenate(
+            [a_ref[2 * v], a_ref[2 * v + 1], a_ref[9 - 2 * v], a_ref[8 - 2 * v]], axis=1
+        )
+        high, low = split(joined)
+        folded = dot(high, fold_ref[...]) + dot(low, fold_ref[...])
+        cut = lat_ref[pl.ds(3, 1), lanes]
+        weight = lat_ref[pl.ds(4, 1), lanes]
+        factors = []
+        for pair in range(5):
+            q = 2 * pair + sub // 4
+            wave = first + q + jnp.where(q >= 5, 635, 0)
+            excess = jnp.maximum(wave.astype(F32) - cut, 0.0) / filter_width
+            doubling = jnp.where(wave == 0, 1.0, 2.0)
+            factors.append(weight * jnp.exp(-0.5 * excess * excess) * doubling)
+        factors = jnp.concatenate(factors * 3 + [jnp.zeros((8, LANES), F32)], axis=0)
+        for parity in range(2):
+            high, low = split(folded[:, parity * LANES : (parity + 1) * LANES] * factors)
+            x_ref[parity, pl.ds(0, 128), lanes] = high
+            x_ref[parity, pl.ds(128, 128), lanes] = low
+
+    acc_ref[...] = jnp.zeros_like(acc_ref)
     geopot = jnp.where(sub % 2 == 0, geo_ref[0], geo_ref[1])
 
-    def analyse(block, parity, buf_ref, update_ref):
+    def analyse(block, parity, update_ref):
         late = block >= CHUNKS // 2
         slot = lane % 8
         upper = slot >= 5
         wave = first + slot + jnp.where(upper, jnp.where(late, 638 - MMAX // 2, 635), 0)
         owner = slot + jnp.where(upper & late, 3, 0)
-        both = dot_t(x_ref[parity], buf_ref[parity, 0])
+        both = dot_t(x_ref[parity], table_ref[block % SLOTS, parity, 0])
         spectral = both[:128] + both[128:] + dot_t(
-            x_ref[parity, pl.ds(0, 128), :], buf_ref[parity, 1]
+            x_ref[parity, pl.ds(0, 128), :], table_ref[block % SLOTS, parity, 1]
         )
         halves = []
         for half in range(2):
@@ -465,34 +505,31 @@
         update_ref[parity, pl.ds(0, 128), :] = high
         update_ref[parity, pl.ds(128, 128), :] = low
 
-    def synthesise(parity, buf_ref, update_ref):
-        both = dot(update_ref[parity], buf_ref[parity, 0])
-        rest = dot(update_ref[parity, pl.ds(0, 128), :], buf_ref[parity, 1])
+    def synthesise(block, parity, update_ref):
+        both = dot(update_ref[parity], table_ref[block % SLOTS, parity, 0])
+        rest = dot(update_ref[parity, pl.ds(0, 128), :], table_ref[block % SLOTS, parity, 1])
         acc_ref[parity] += both[:128] + both[128:] + rest
 
-    tables = (table0_ref, table1_ref, table2_ref)
-    updates = (update0_ref, update1_ref, update2_ref)
-    generate(0, tables[0])
-    generate(1, tables[1])
+    arrived(0)
     for parity in range(2):
-        analyse(0, parity, tables[0], updates[0])
-
-    @pl.loop(0, (CHUNKS + 2) // 3)
-    def _(group):
-        for turn in range(3):
-            block = 3 * group + turn
-
-            def advance(block=block, turn=turn):
-                now, later, last = turn, (turn + 1) % 3, (turn + 2) % 3
-                generate(block + 2, tables[last])
-                for parity in range(2):
-                    analyse(block + 1, parity, tables[later], updates[later])
-                    synthesise(parity, tables[now], updates[now])
-
-            if turn < 2:
-                advance()
-            else:
-                pl.when(block < CHUNKS)(advance)
+        analyse(0, parity, update0_ref)
+
+    @pl.loop(0, CHUNKS // 2 - 1)
+    def _(pair):
+        for turn, (now, later) in enumerate(((update0_ref, update1_ref), (update1_ref, update0_ref))):
+            block = 2 * pair + turn
+            arrived(block + 1)
+            fetch(block + 3)
+            for parity in range(2):
+                analyse(2 * pair + turn + 1, parity, later)
+                synthesise(2 * pair + turn, parity, now)
+
+    arrived(CHUNKS - 1)
+    for parity in range(2):
+        analyse(CHUNKS - 1, parity, update1_ref)
+        synthesise(CHUNKS - 2, parity, update0_ref)
+    for parity in range(2):
+        synthesise(CHUNKS - 1, parity, update1_ref)
 
     for v in range(TILES):
         lanes = pl.ds(v * LANES, LANES)
@@ -507,10 +544,11 @@
 
 VMEM = pl.BlockSpec(memory_space=pltpu.VMEM)
 SMEM = pl.BlockSpec(memory_space=pltpu.SMEM)
-
-
-def call(kernel, outputs, specs, scratch, megabytes, flops, name):
-    shapes = tuple(jax.ShapeDtypeStruct(shape, F32) for shape in outputs)
+HBM = pl.BlockSpec(memory_space=pltpu.HBM)
+
+
+def call(kernel, outputs, specs, scratch, megabytes, flops, name, dtype=F32):
+    shapes = tuple(jax.ShapeDtypeStruct(shape, dtype) for shape in outputs)
     single = len(shapes) == 1
     return pl.pallas_call(
         kernel,
@@ -524,14 +562,49 @@
     )
 
 
+def table_call(phase, rank, logs, lat, before):
+    def whole(*shape):
+        return pl.BlockSpec(shape, lambda step: (0,) * len(shape))
+
+    return pl.pallas_call(
+        functools.partial(table_kernel, phase),
+        grid=(HALF,),
+        out_shape=(
+            pltpu.HBM((HALF, 2, 2, 256, 640), BF16),
+            jax.ShapeDtypeStruct((3, 8, 640), F32),
+        ),
+        in_specs=[SMEM, SMEM, whole(8, 640), whole(3, 8, 640)],
+        out_specs=(
+            pl.BlockSpec((1, 2, 2, 256, 640), lambda step: (step, 0, 0, 0, 0)),
+            whole(3, 8, 640),
+        ),
+        scratch_shapes=[pltpu.VMEM((HALF, 2, 8, LANES), F32)],
+        compiler_params=pltpu.CompilerParams(vmem_limit_bytes=12 << 20),
+        cost_estimate=pl.CostEstimate(flops=1 << 32, bytes_accessed=13 << 20, transcendentals=0),
+        name="table",
+    )(rank, logs, lat, before)
+
+
 def shards(vorticity, divergence, height, mean_geopot):
     rank = lax.axis_index("lat") * lax.axis_size("lon") + lax.axis_index("lon")
     rank = rank.astype(jnp.int32).reshape(1)
     twiddle = jnp.asarray(twiddles())
-    packed = call(pack_kernel, [(4, 64, 640)], [VMEM] * 3, [], 8, 1 << 20, "pack")(
-        vorticity, divergence, height
+    packed = call(
+        pack_kernel,
+        [(4, 64, 640)],
+        [HBM] * 3,
+        [pltpu.VMEM((2, 40, 640), F32) for _ in range(3)] + [pltpu.SemaphoreType.DMA((3,))],
+        8,
+        1 << 20,
+        "pack",
+    )(
+        *(pltpu.with_memory_space_constraint(x, pltpu.HBM) for x in (vorticity, divergence, height))
     )
+    lat = jnp.asarray(latitude_rows())
+    logs = jnp.asarray(sector_logs())
+    early, state = table_call(0, rank, logs, lat, jnp.zeros((3, 8, 640), F32))
     sectors = lax.all_to_all(packed, "lon", split_axis=0, concat_axis=0, tiled=True)
+    sectors, state = lax.optimization_barrier((sectors, state))
     spectrum = call(
         forward_kernel,
         [(128, 1280)],
@@ -541,33 +614,35 @@
         1 << 28,
         "forward",
     )(sectors, twiddle, jnp.asarray(forward_matrix()))
+    spectrum, state = lax.optimization_barrier((spectrum, state))
+    late, _ = table_call(1, rank, logs, lat, state)
     columns = lax.all_to_all(spectrum, ("lat", "lon"), split_axis=0, concat_axis=0, tiled=True)
     synthesis = call(
         legendre_kernel,
         [(128, 1280)],
-        [SMEM] * 3 + [VMEM] * 5,
+        [SMEM] * 2 + [VMEM] * 5 + [HBM] * 2,
         [
             pltpu.VMEM((10, 128, LANES), F32),
             pltpu.VMEM((2, 256, 640), BF16),
-            pltpu.VMEM((CHUNKS + 3, 2, 8, LANES), F32),
-            pltpu.VMEM((3, 8, 640), F32),
-            pltpu.VMEM((2, 2, 8, 640), F32),
-            *[pltpu.VMEM((2, 2, 256, 640), BF16) for _ in range(3)],
-            *[pltpu.VMEM((2, 256, 256), BF16) for _ in range(3)],
+            pltpu.VMEM((2, 256, 256), BF16),
+            pltpu.VMEM((2, 256, 256), BF16),
             pltpu.VMEM((2, 128, 640), F32),
+            pltpu.VMEM((SLOTS, 2, 2, 256, 640), BF16),
+            pltpu.SemaphoreType.DMA((SLOTS,)),
         ],
-        32,
+        20,
         1 << 33,
         "legendre",
     )(
         rank,
-        jnp.asarray(sector_logs()),
         mean_geopot,
         columns,
-        jnp.asarray(latitude_rows()),
+        lat,
         jnp.asarray(gather_matrix()),
         jnp.asarray(fold_matrix()),
         jnp.asarray(unfold_matrix()),
+        pltpu.with_memory_space_constraint(early, pltpu.HBM),
+        pltpu.with_memory_space_constraint(late, pltpu.HBM),
     )
     gathered = lax.all_to_all(synthesis, ("lat", "lon"), split_axis=0, concat_axis=0, tiled=True)
     result = call(

time: 112 us -> 107 us (0.955)
  blocking collectives: 50.6 us -> 33.5 us
  Pallas kernels: 31.1 us -> 47.1 us
  waiting for transfers between devices: 14.6 us -> 4.86 us
  starting transfers between devices: 8.01 us -> 16.3 us
  local copies, waits for them, and re-layouts: 6.72 us -> 3.76 us
    all_to_all x1 -> x0, blocking collectives: 17.3 us -> none  [shards(): lax.all_to_all(packed, 'lon', split_axis=0, concat_axis=0, tiled=True)]
    pallas_call x2 -> x4, Pallas kernels: 26.1 us -> 42.1 us  [the longest x1 20.3 us: shards(): call(legendre_kernel, [(128, 1280)], [SMEM] * 2 + [VMEM] * 5 + [HBM] * 2,...]
    all_to_all x1, waiting for transfers between devices: 14.6 us -> 4.86 us  [shards(): lax.all_to_all(spectrum, ('lat', 'lon'), split_axis=0, concat_axis=0, til...]
    all_to_all x0 -> x1, starting transfers between devices: none -> 6.66 us  [shards(): lax.all_to_all(packed, 'lon', split_axis=0, concat_axis=0, tiled=True)]
    unnamed x28 -> x26, local copies, waits for them, and re-layouts: 4.51 us -> 1.56 us
    all_to_all x1, starting transfers between devices: 8.01 us -> 9.65 us  [shards(): lax.all_to_all(spectrum, ('lat', 'lon'), split_axis=0, concat_axis=0, til...]
  transfers between devices with their start and end apart: 1 -> 2, of which waited for: 1 -> 1; matrix products, arithmetic and copies ran while one was open for 0% -> 0% of each run, Pallas kernels for 0% -> 19%
where the time goes in v3:
time: 107 us; the launch traced here: 106 us
  Pallas kernels  47.1 us (44%)
  blocking collectives  33.5 us (31%)
  starting transfers between devices  16.3 us (15%)
  waiting for transfers between devices  4.86 us (5%)
  local copies, waits for them, and re-layouts  3.76 us (4%)
    pallas_call x1, Pallas kernels, shards(): call(legendre_kernel, [(128, 1280)], [SMEM] * 2 + [VMEM] * 5 + [HBM] * 2,...  20.3 us
    pallas_call x2, Pallas kernels, table_call(): pl.pallas_call(functools.partial(table_kernel, phase), grid=(HALF,), out_...  19.7 us
    all_to_all x1, blocking collectives, shards(): lax.all_to_all(synthesis, ('lat', 'lon'), split_axis=0, concat_axis=0, ti...  19.5 us
    all_to_all x1, blocking collectives, shards(): lax.all_to_all(result, 'lon', split_axis=0, concat_axis=0, tiled=True)  14 us
    all_to_all x1, starting transfers between devices, shards(): lax.all_to_all(spectrum, ('lat', 'lon'), split_axis=0, concat_axis=0, til...  9.65 us
    all_to_all x1, starting transfers between devices, shards(): lax.all_to_all(packed, 'lon', split_axis=0, concat_axis=0, tiled=True)  6.66 us
    all_to_all x1, waiting for transfers between devices, shards(): lax.all_to_all(spectrum, ('lat', 'lon'), split_axis=0, concat_axis=0, til...  4.86 us
    pallas_call x1, Pallas kernels, shards(): call(inverse_kernel, [(4, 64, 640)], [VMEM] * 4, [pltpu.VMEM((4, 5, 64, L...  2.81 us
  transfers between devices with their start and end apart: 2, of which 1 were waited for; matrix products, arithmetic and copies ran while one was open for 0% of the time, Pallas kernels for 19%

profile of v3, /device:TPU:1, one launch (start us, length us, event | category | flops | bytes accessed | tf_op | source)
XLA Modules:
  0.0 106.4 jit_solution(15441700903252369885)
XLA Ops:
  0.6 0.0 copy-start.9
  0.6 0.0 copy-start.11
  0.7 0.0 copy-start.1
  0.7 0.0 copy-start.2
  0.7 2.1 %pack.1 = f32[4,64,640]{2,1,0:T(8,128)} custom-call(f32[2,40,640]{2,1,0:T(8,128)} %vort_hbm.1, f32[2,40,640]{2,1,0:T(8,128)} %div_hbm.1, f32[2,40,640]{2,1,0:T(8,128)} %height_hbm.1), custom_call_target="tpu_custom_call" | custom-call | flops 1048576 | bytes 2097152 | tf_op jit(solution)/shard_map/pack/pallas_call | solution.py:592
  2.8 6.7 %all-to-all-start = ((f32[4,64,640]{2,1,0:T(8,128)}), f32[4,64,640]{2,1,0:T(8,128)S(1)}, u32[]{:S(2)}, u32[]{:S(2)}) async-start(f32[4,64,640]{2,1,0:T(8,128)} %pack.1), calls=%async_computation | async-start | bytes 1310720 | tf_op jit(solution)/shard_map/all_to_all | solution.py:606
  9.4 0.0 copy-start.8
  9.4 0.7 copy-done.8
  10.2 0.0 copy-start.10
  10.2 0.7 copy-done.10
  10.8 9.9 %table.2 = (bf16[10,2,2,256,640]{4,3,2,1,0:T(8,128)(2,1)}, f32[3,8,640]{2,1,0:T(8,128)S(1)}) custom-call(s32[1]{0:T(128)} %bitcast.rank_ref, f32[1280]{0:T(1024)S(1)} %copy-done.10, f32[8,640]{1,0:T(8,128)S(1)} %copy-done.8, f32[3,8,640]{2,1,0:T(8,128)S(1)} %broadcast_in_dim.3.before_ref), custom_call_target="tpu_custom_call" | custom-call | flops 4294967296 | bytes 13631488 | tf_op jit(solution)/shard_map/table/pallas_call | solution.py:569
  20.7 0.0 copy-start.4
  20.7 0.0 copy-start.5
  20.7 0.0 copy-start.6
  20.7 0.0 copy-start.7
  20.7 0.0 all-to-all-done.in_ref
  20.7 0.0 copy-done.1
  20.7 0.0 copy-done.2
  20.8 1.3 %forward.1 = f32[128,1280]{1,0:T(8,128)S(1)} custom-call(f32[4,64,640]{2,1,0:T(8,128)S(1)} %all-to-all-done.in_ref, f32[40,128]{1,0:T(8,128)S(1)} %copy-done.1, bf16[128,256]{1,0:T(8,128)(2,1)S(1)} %copy-done.2), custom_call_target="tpu_custom_call" | custom-call | flops 268435456 | bytes 2097152 | tf_op jit(solution)/shard_map/forward/pallas_call | solution.py:608
  22.0 1.5 %copy.16 = f32[128,1,1280]{2,1,0:T(1,128)} copy(f32[128,1,1280]{2,0,1:T(8,128)S(1)} %bitcast.9) | data formatting | bytes 1310720 | tf_op jit(solution)/shard_map/all_to_all | solution.py:619
  23.6 9.7 %all-to-all-start.1 = ((f32[128,1,1280]{2,1,0:T(1,128)}), f32[128,1,1280]{2,1,0:T(1,128)S(1)}, u32[]{:S(2)}, u32[]{:S(2)}) async-start(f32[128,1,1280]{2,1,0:T(1,128)} %copy.16), calls=%async_computation.1 | async-start | bytes 1310720 | tf_op jit(solution)/shard_map/all_to_all | solution.py:619
  33.2 0.0 copy-done.9
  33.2 0.0 copy-done.11
  33.2 9.8 %table.3 = (bf16[10,2,2,256,640]{4,3,2,1,0:T(8,128)(2,1)}, f32[3,8,640]{2,1,0:T(8,128)}) custom-call(s32[1]{0:T(128)} %bitcast.rank_ref, f32[1280]{0:T(1024)S(1)} %copy-done.11, f32[8,640]{1,0:T(8,128)S(1)} %copy-done.9, f32[3,8,640]{2,1,0:T(8,128)S(1)} %get-tuple-element.15.before_ref), custom_call_target="tpu_custom_call" | custom-call | flops 4294967296 | bytes 13631488 | tf_op jit(solution)/shard_map/table/pallas_call | solution.py:569
  43.1 4.9 %all-to-all-done.1 = f32[128,1,1280]{2,1,0:T(1,128)S(1)} async-done(((f32[128,1,1280]{2,1,0:T(1,128)}), f32[128,1,1280]{2,1,0:T(1,128)S(1)}, u32[]{:S(2)}, u32[]{:S(2)}) %all-to-all-start.1) | async-done | bytes 655392 | tf_op jit(solution)/shard_map/all_to_all | solution.py:619
  48.0 0.0 copy-done.4
  48.0 0.0 copy-done.5
  48.0 0.0 copy-done.6
  48.0 0.0 copy-done.7
  48.0 0.0 copy-start
  48.0 0.0 copy-start.3
  48.0 20.3 %legendre.1 = f32[128,1280]{1,0:T(8,128)S(1)} custom-call(s32[1]{0:T(128)} %bitcast.rank_ref, f32[2]{0:T(128)S(1)} %copy-done.4, f32[128,1280]{1,0:T(8,128)S(1)} %bitcast.11, f32[8,640]{1,0:T(8,128)S(1)} %copy-done.9, bf16[240,256]{1,0:T(8,128)(2,1)S(1)} %copy-done.7, bf16[512,256]{1,0:T(8,128)(2,1)S(1)} %copy-done.5, bf16[256,256]{1,0:T(8,128)(2,1)S(1)} %copy-done.6, ...), custom_call_target="tpu_custom_call" | custom-call | flops 8589934592 | bytes 2097152 | tf_op jit(solution)/shard_map/legendre/pallas_call | solution.py:620
  68.4 0.7 copy.17
  69.1 19.5 %all_to_all.32 = f32[128,1,1280]{2,1,0:T(1,128)S(1)} all-to-all(f32[128,1,1280]{2,1,0:T(1,128)S(1)} %copy.17), channel_id=1, replica_groups=mesh['lat'=32,'lon'=4] {'lat','lon'}, dimensions={0} | all-to-all | bytes 1310720 | tf_op jit(solution)/shard_map/all_to_all | solution.py:647
  88.6 0.0 copy-done
  88.6 0.0 copy-done.3
  88.6 2.8 %inverse.1 = f32[4,64,640]{2,1,0:T(8,128)S(1)} custom-call(f32[128,1280]{1,0:T(8,128)S(1)} %bitcast.10, bf16[160,128]{1,0:T(8,128)(2,1)S(1)} %copy-done.3, f32[40,128]{1,0:T(8,128)S(1)} %copy-done.1, bf16[1024,256]{1,0:T(8,128)(2,1)S(1)} %copy-done), custom_call_target="tpu_custom_call" | custom-call | flops 268435456 | bytes 2097152 | tf_op jit(solution)/shard_map/inverse/pallas_call | solution.py:648
  91.4 14.0 %all_to_all.33.in_ref = f32[4,64,640]{2,1,0:T(8,128)S(1)} all-to-all(f32[4,64,640]{2,1,0:T(8,128)S(1)} %inverse.1), channel_id=1, replica_groups=mesh['lat'=32,'lon'=4] {'lon'}, dimensions={0} | all-to-all | bytes 1310720 | tf_op jit(solution)/shard_map/all_to_all | solution.py:657
  105.5 0.9 unpack.1
  (3 shorter events, 0.1 us)
Async XLA Ops:
  0.6 32.6 %copy-start.9 = (f32[8,640]{1,0:T(8,128)S(1)}, f32[8,640]{1,0:T(8,128)}, u32[]{:S(2)}) copy-start(f32[8,640]{1,0:T(8,128)} %constant.32.clone.lat_ref) | copy-start | bytes 61444
  0.6 32.6 %copy-start.11 = (f32[1280]{0:T(1024)S(1)}, f32[1280]{0:T(1024)}, u32[]{:S(2)}) copy-start(f32[1280]{0:T(1024)} %constant.33.clone.logs_ref) | copy-start | bytes 15364
  0.7 20.1 %copy-start.1 = (f32[40,128]{1,0:T(8,128)S(1)}, f32[40,128]{1,0:T(8,128)}, u32[]{:S(2)}) copy-start(f32[40,128]{1,0:T(8,128)} %constant.31.clone.twiddle_ref) | copy-start | bytes 61444
  0.7 20.1 %copy-start.2 = (bf16[128,256]{1,0:T(8,128)(2,1)S(1)}, bf16[128,256]{1,0:T(8,128)(2,1)}, u32[]{:S(2)}) copy-start(bf16[128,256]{1,0:T(8,128)(2,1)} %constant.34.clone.table_ref) | copy-start | bytes 196612
  2.8 18.0 %all-to-all-start = ((f32[4,64,640]{2,1,0:T(8,128)}), f32[4,64,640]{2,1,0:T(8,128)S(1)}, u32[]{:S(2)}, u32[]{:S(2)}) async-start(f32[4,64,640]{2,1,0:T(8,128)} %pack.1), calls=%async_computation | async-start | bytes 1310720 | tf_op jit(solution)/shard_map/all_to_all | solution.py:606
  9.4 0.7 copy-start.8
  10.2 0.7 copy-start.10
  20.7 27.3 %copy-start.4 = (f32[2]{0:T(128)S(1)}, f32[2]{0:T(128)}, u32[]{:S(2)}) copy-start(f32[2]{0:T(128)} %geo_ref.1) | copy-start | bytes 28
  20.7 27.3 %copy-start.5 = (bf16[512,256]{1,0:T(8,128)(2,1)S(1)}, bf16[512,256]{1,0:T(8,128)(2,1)}, u32[]{:S(2)}) copy-start(bf16[512,256]{1,0:T(8,128)(2,1)} %constant.36.clone.fold_ref) | copy-start | bytes 786436
  20.7 27.3 %copy-start.6 = (bf16[256,256]{1,0:T(8,128)(2,1)S(1)}, bf16[256,256]{1,0:T(8,128)(2,1)}, u32[]{:S(2)}) copy-start(bf16[256,256]{1,0:T(8,128)(2,1)} %constant.37.clone.unfold_ref) | copy-start | bytes 393220
  20.7 27.3 %copy-start.7 = (bf16[240,256]{1,0:T(8,128)(2,1)S(1)}, bf16[240,256]{1,0:T(8,128)(2,1)}, u32[]{:S(2)}) copy-start(bf16[240,256]{1,0:T(8,128)(2,1)} %constant.35.clone.gather_ref) | copy-start | bytes 368644
  23.6 24.4 %all-to-all-start.1 = ((f32[128,1,1280]{2,1,0:T(1,128)}), f32[128,1,1280]{2,1,0:T(1,128)S(1)}, u32[]{:S(2)}, u32[]{:S(2)}) async-start(f32[128,1,1280]{2,1,0:T(1,128)} %copy.16), calls=%async_computation.1 | async-start | bytes 1310720 | tf_op jit(solution)/shard_map/all_to_all | solution.py:619
  48.0 40.6 %copy-start = (bf16[1024,256]{1,0:T(8,128)(2,1)S(1)}, bf16[1024,256]{1,0:T(8,128)(2,1)}, u32[]{:S(2)}) copy-start(bf16[1024,256]{1,0:T(8,128)(2,1)} %constant.39.clone.table_ref) | copy-start | bytes 1572868
  48.0 40.6 %copy-start.3 = (bf16[160,128]{1,0:T(8,128)(2,1)S(1)}, bf16[160,128]{1,0:T(8,128)(2,1)}, u32[]{:S(2)}) copy-start(bf16[160,128]{1,0:T(8,128)(2,1)} %constant.38.clone.scatter_ref) | copy-start | bytes 122884

commit v4 on v3

--- a/solution.py
+++ b/solution.py
@@ -147,11 +147,32 @@
 S1, S2 = float(np.sin(2 * np.pi / 5)), float(np.sin(4 * np.pi / 5))
 
 
-def pack_kernel(vort_hbm, div_hbm, height_hbm, out_ref, vort_ref, div_ref, height_ref, sem_ref):
+def pack_kernel(
+    rank_ref,
+    logs_hbm,
+    lat_hbm,
+    vort_hbm,
+    div_hbm,
+    height_hbm,
+    out_ref,
+    start_ref,
+    lat_ref,
+    vort_ref,
+    div_ref,
+    height_ref,
+    logs_ref,
+    sem_ref,
+):
     copies = [
         pltpu.make_async_copy(source, target, sem_ref.at[index])
         for index, (source, target) in enumerate(
-            ((vort_hbm, vort_ref), (div_hbm, div_ref), (height_hbm, height_ref))
+            (
+                (vort_hbm, vort_ref),
+                (div_hbm, div_ref),
+                (height_hbm, height_ref),
+                (logs_hbm, logs_ref),
+                (lat_hbm, lat_ref),
+            )
         )
     ]
     for copy in copies:
@@ -163,13 +184,34 @@
         for b in range(4):
             for lev in range(2):
                 out_ref[b, pl.ds((2 * f + lev) * 10, 10), :] = ref[lev, pl.ds(10 * b, 10), :]
-
-
-def unpack_kernel(in_ref, vort_ref, div_ref, height_ref):
-    for b in range(4):
-        for f, ref in enumerate((vort_ref, div_ref, height_ref)):
-            for lev in range(2):
-                ref[lev, pl.ds(10 * b, 10), :] = in_ref[b, pl.ds((2 * f + lev) * 10, 10), :]
+    copies[3].wait()
+    copies[4].wait()
+    rank = rank_ref[0]
+    first = (rank % 32) * 20 + (rank // 32) * 5
+    sub = lax.broadcasted_iota(jnp.int32, (8, LANES), 0)
+    for phase in range(2):
+        logs = jnp.zeros((8, LANES), F32)
+        for slot in range(8):
+            offset = min(slot + (635 + 3 * phase if slot >= 5 else 0), 644)
+            logs = jnp.where(sub == slot, logs_ref[first + offset], logs)
+        start_ref[phase] = logs
+
+
+def unpack_kernel(
+    rank_ref, in0_ref, in1_ref, in2_ref, in3_ref, vort_ref, div_ref, height_ref
+):
+    pieces = (in0_ref, in1_ref, in2_ref, in3_ref)
+
+    def place(lon):
+        for b in range(4):
+            for f, ref in enumerate((vort_ref, div_ref, height_ref)):
+                for lev in range(2):
+                    ref[lev, pl.ds(10 * b, 10), :] = pieces[(lon - b) % 4][
+                        pl.ds((2 * f + lev) * 10, 10), :
+                    ]
+
+    for lon in range(4):
+        pl.when(rank_ref[0] % 4 == lon)(functools.partial(place, lon))
 
 
 def forward_kernel(in_ref, twiddle_ref, table_ref, out_ref, z_ref):
@@ -237,7 +279,20 @@
             ]
 
 
-def inverse_kernel(in_ref, scatter_ref, twiddle_ref, table_ref, out_ref, c_ref, z_ref):
+def inverse_kernel(
+    rank_ref,
+    in_ref,
+    scatter_ref,
+    twiddle_ref,
+    table_ref,
+    out0_ref,
+    out1_ref,
+    out2_ref,
+    out3_ref,
+    c_ref,
+    z_ref,
+    out_ref,
+):
     for part in range(4):
         for i in range(5):
             c_ref[part, i, pl.ds(56, 8), :] = jnp.zeros((8, LANES), F32)
@@ -291,8 +346,22 @@
                 i2 = (4 * n5 + 5 * n4) % 20
                 out_ref[i2 // 5, rows, pl.ds((i2 % 5) * 128, 128)] = value
 
-
-def table_kernel(phase, rank_ref, logs_ref, lat_ref, before_ref, table_ref, state_ref, coef_ref):
+    for shift, piece_ref in enumerate((out0_ref, out1_ref, out2_ref, out3_ref)):
+        piece_ref[...] = out_ref[(rank_ref[0] + shift) % 4]
+
+
+def table_kernel(
+    phase,
+    rank_ref,
+    logs_ref,
+    lat_ref,
+    before_ref,
+    table_ref,
+    state_ref,
+    coef_ref,
+    buf_ref,
+    sem_ref,
+):
     rank = rank_ref[0]
     first = (rank % 32) * 20 + (rank // 32) * 5
     sub = lax.broadcasted_iota(jnp.int32, (8, LANES), 0)
@@ -305,11 +374,7 @@
         fresh = (sub >= 5) | (phase == 0)
         shift = jnp.where(sub >= 5, 635 + 3 * phase, 0)
         wave = (first + sub + shift).astype(F32)
-        logs = jnp.zeros((8, LANES), F32)
-        for slot in range(8):
-            offset = slot + (635 + 3 * phase if slot >= 5 else 0)
-            offset = min(offset, 644)
-            logs = jnp.where(sub == slot, logs_ref[first + offset], logs)
+        logs = logs_ref[phase]
         for v in range(TILES):
             lanes = pl.ds(v * LANES, LANES)
             main = wave * lat_ref[pl.ds(1, 1), lanes]
@@ -341,6 +406,22 @@
             return 0
 
         lax.fori_loop(0, HALF, coefficients, 0)
+
+    slot = step_index % 2
+
+    def copies(step):
+        return [
+            pltpu.make_async_copy(
+                buf_ref.at[step % 2, part // 2, part % 2],
+                table_ref.at[step, part // 2, part % 2],
+                sem_ref.at[step % 2, part],
+            )
+            for part in range(4)
+        ]
+
+    def finish(step):
+        for copy in copies(step):
+            copy.wait()
 
     def generate():
         newer, older, power, scale, cosine = [], [], [], [], []
@@ -378,15 +459,23 @@
                             [held.pop((t - 3 + parity, v)), held.pop((t - 1 + parity, v))], axis=0
                         )
                         high, low = split(both)
-                        table_ref[0, parity, 0, rows, lanes] = high
-                        table_ref[0, parity, 1, rows, lanes] = low
+                        buf_ref[slot, parity, 0, rows, lanes] = high
+                        buf_ref[slot, parity, 1, rows, lanes] = low
         for v in range(TILES):
             lanes = pl.ds(v * LANES, LANES)
             state_ref[0, :, lanes] = newer[v]
             state_ref[1, :, lanes] = older[v]
             state_ref[2, :, lanes] = power[v]
 
+    pl.when(step_index >= 2)(lambda: finish(step_index - 2))
     generate()
+    for copy in copies(step_index):
+        copy.start()
+
+    @pl.when(step_index == HALF - 1)
+    def _():
+        finish(HALF - 2)
+        finish(HALF - 1)
 
 
 def legendre_kernel(
@@ -413,22 +502,32 @@
     sub = lax.broadcasted_iota(jnp.int32, (8, LANES), 0)
     lane = lax.broadcasted_iota(jnp.int32, (8, LANES), 1)
 
+    def pieces(source_ref, index, slot):
+        return [
+            pltpu.make_async_copy(
+                source_ref.at[index, part // 2, part % 2],
+                table_ref.at[slot, part // 2, part % 2],
+                sem_ref.at[slot, part],
+            )
+            for part in range(4)
+        ]
+
     def fetch(block):
         slot = block % SLOTS
 
         @pl.when(block < HALF)
         def _():
-            pltpu.make_async_copy(early_ref.at[block], table_ref.at[slot], sem_ref.at[slot]).start()
+            for copy in pieces(early_ref, block, slot):
+                copy.start()
 
         @pl.when((block >= HALF) & (block < CHUNKS))
         def _():
-            pltpu.make_async_copy(
-                late_ref.at[block - HALF], table_ref.at[slot], sem_ref.at[slot]
-            ).start()
+            for copy in pieces(late_ref, block - HALF, slot):
+                copy.start()
 
     def arrived(block):
-        slot = block % SLOTS
-        pltpu.make_async_copy(early_ref.at[0], table_ref.at[slot], sem_ref.at[slot]).wait()
+        for copy in pieces(early_ref, 0, block % SLOTS):
+            copy.wait()
 
     for block in range(3):
         fetch(block)
@@ -537,7 +636,7 @@
         high, low = split(joined)
         moved = dot_t(unfold_ref[...], high) + dot_t(unfold_ref[...], low)
         for part, u in enumerate((2 * v, 2 * v + 1, 9 - 2 * v, 8 - 2 * v)):
-            out_ref[pl.ds((part // 2) * 64, 64), pl.ds(u * LANES, LANES)] = moved[
+            out_ref[pl.ds(64 - (part // 2) * 64, 64), pl.ds(u * LANES, LANES)] = moved[
                 part * 64 : part * 64 + 64
             ]
 
@@ -573,12 +672,16 @@
             pltpu.HBM((HALF, 2, 2, 256, 640), BF16),
             jax.ShapeDtypeStruct((3, 8, 640), F32),
         ),
-        in_specs=[SMEM, SMEM, whole(8, 640), whole(3, 8, 640)],
+        in_specs=[SMEM, whole(2, 8, LANES), whole(8, 640), whole(3, 8, 640)],
         out_specs=(
-            pl.BlockSpec((1, 2, 2, 256, 640), lambda step: (step, 0, 0, 0, 0)),
+            HBM,
             whole(3, 8, 640),
         ),
-        scratch_shapes=[pltpu.VMEM((HALF, 2, 8, LANES), F32)],
+        scratch_shapes=[
+            pltpu.VMEM((HALF, 2, 8, LANES), F32),
+            pltpu.VMEM((2, 2, 2, 256, 640), BF16),
+            pltpu.SemaphoreType.DMA((2, 4)),
+        ],
         compiler_params=pltpu.CompilerParams(vmem_limit_bytes=12 << 20),
         cost_estimate=pl.CostEstimate(flops=1 << 32, bytes_accessed=13 << 20, transcendentals=0),
         name="table",
@@ -589,19 +692,17 @@
     rank = lax.axis_index("lat") * lax.axis_size("lon") + lax.axis_index("lon")
     rank = rank.astype(jnp.int32).reshape(1)
     twiddle = jnp.asarray(twiddles())
-    packed = call(
+    sources = (jnp.asarray(sector_logs()), jnp.asarray(latitude_rows()), vorticity, divergence, height)
+    packed, logs, lat = call(
         pack_kernel,
-        [(4, 64, 640)],
-        [HBM] * 3,
-        [pltpu.VMEM((2, 40, 640), F32) for _ in range(3)] + [pltpu.SemaphoreType.DMA((3,))],
+        [(4, 64, 640), (2, 8, LANES), (8, 640)],
+        [SMEM] + [HBM] * 5,
+        [pltpu.VMEM((2, 40, 640), F32) for _ in range(3)]
+        + [pltpu.SMEM((MMAX,), F32), pltpu.SemaphoreType.DMA((5,))],
         8,
         1 << 20,
         "pack",
-    )(
-        *(pltpu.with_memory_space_constraint(x, pltpu.HBM) for x in (vorticity, divergence, height))
-    )
-    lat = jnp.asarray(latitude_rows())
-    logs = jnp.asarray(sector_logs())
+    )(rank, *(pltpu.with_memory_space_constraint(x, pltpu.HBM) for x in sources))
     early, state = table_call(0, rank, logs, lat, jnp.zeros((3, 8, 640), F32))
     sectors = lax.all_to_all(packed, "lon", split_axis=0, concat_axis=0, tiled=True)
     sectors, state = lax.optimization_barrier((sectors, state))
@@ -628,7 +729,7 @@
             pltpu.VMEM((2, 256, 256), BF16),
             pltpu.VMEM((2, 128, 640), F32),
             pltpu.VMEM((SLOTS, 2, 2, 256, 640), BF16),
-            pltpu.SemaphoreType.DMA((SLOTS,)),
+            pltpu.SemaphoreType.DMA((SLOTS, 4)),
         ],
         20,
         1 << 33,
@@ -647,15 +748,30 @@
     gathered = lax.all_to_all(synthesis, ("lat", "lon"), split_axis=0, concat_axis=0, tiled=True)
     result = call(
         inverse_kernel,
-        [(4, 64, 640)],
-        [VMEM] * 4,
-        [pltpu.VMEM((4, 5, 64, LANES), F32), pltpu.VMEM((20, 64, 256), F32)],
+        [(64, 640)] * 4,
+        [SMEM] + [VMEM] * 4,
+        [
+            pltpu.VMEM((4, 5, 64, LANES), F32),
+            pltpu.VMEM((20, 64, 256), F32),
+            pltpu.VMEM((4, 64, 640), F32),
+        ],
         16,
         1 << 28,
         "inverse",
-    )(gathered, jnp.asarray(scatter_matrix()), twiddle, jnp.asarray(inverse_matrix()))
-    pieces = lax.all_to_all(result, "lon", split_axis=0, concat_axis=0, tiled=True)
-    return call(unpack_kernel, [(2, 40, 640)] * 3, [VMEM], [], 8, 1 << 20, "unpack")(pieces)
+    )(rank, gathered, jnp.asarray(scatter_matrix()), twiddle, jnp.asarray(inverse_matrix()))
+    n_lat = lax.axis_size("lat")
+    n_lon = lax.axis_size("lon")
+    pieces = []
+    for shift, piece in enumerate(result):
+        pairs = [
+            (lat_at * n_lon + lon_at, (lat_at ^ 16) * n_lon + (lon_at + shift) % n_lon)
+            for lat_at in range(n_lat)
+            for lon_at in range(n_lon)
+        ]
+        pieces.append(lax.ppermute(piece, ("lat", "lon"), pairs))
+    return call(unpack_kernel, [(2, 40, 640)] * 3, [SMEM] + [VMEM] * 4, [], 8, 1 << 20, "unpack")(
+        rank, *pieces
+    )
 
 
 def solution(mesh):

time: 107 us -> 103 us (0.963)
  blocking collectives: 33.5 us -> 19.4 us
  waiting for transfers between devices: 4.86 us -> 14.4 us
  starting transfers between devices: 16.3 us -> 18.6 us
  local copies, waits for them, and re-layouts: 3.76 us -> 2.35 us
    all_to_all x1 -> x0, blocking collectives: 14 us -> none  [shards(): lax.all_to_all(result, 'lon', split_axis=0, concat_axis=0, tiled=True)]
    ppermute x0 -> x4, waiting for transfers between devices: none -> 7.96 us  [shards(): pieces.append(lax.ppermute(piece, ('lat', 'lon'), pairs))]
    ppermute x0 -> x4, starting transfers between devices: none -> 3.88 us  [shards(): pieces.append(lax.ppermute(piece, ('lat', 'lon'), pairs))]
    all_to_all x1, waiting for transfers between devices: 0.01 us -> 1.58 us  [shards(): lax.all_to_all(packed, 'lon', split_axis=0, concat_axis=0, tiled=True)]
    all_to_all x1, starting transfers between devices: 9.65 us -> 8.1 us  [shards(): lax.all_to_all(spectrum, ('lat', 'lon'), split_axis=0, concat_axis=0, til...]
    unnamed x26 -> x18, local copies, waits for them, and re-layouts: 1.56 us -> 0.14 us
  transfers between devices with their start and end apart: 2 -> 6, of which waited for: 1 -> 6; matrix products, arithmetic and copies ran while one was open for 0% -> 0% of each run, Pallas kernels for 19% -> 19%
where the time goes in v4:
time: 103 us
  Pallas kernels  46.9 us (46%)
  blocking collectives  19.4 us (19%)
  starting transfers between devices  18.6 us (18%)
  waiting for transfers between devices  14.4 us (14%)
  local copies, waits for them, and re-layouts  2.35 us (2%)
    pallas_call x1, Pallas kernels, shards(): call(legendre_kernel, [(128, 1280)], [SMEM] * 2 + [VMEM] * 5 + [HBM] * 2,...  20.7 us
    all_to_all x1, blocking collectives, shards(): lax.all_to_all(synthesis, ('lat', 'lon'), split_axis=0, concat_axis=0, ti...  19.4 us
    pallas_call x2, Pallas kernels, table_call(): pl.pallas_call(functools.partial(table_kernel, phase), grid=(HALF,), out_...  19.1 us
    all_to_all x1, starting transfers between devices, shards(): lax.all_to_all(spectrum, ('lat', 'lon'), split_axis=0, concat_axis=0, til...  8.1 us
    ppermute x4, waiting for transfers between devices, shards(): pieces.append(lax.ppermute(piece, ('lat', 'lon'), pairs))  7.96 us
    all_to_all x1, starting transfers between devices, shards(): lax.all_to_all(packed, 'lon', split_axis=0, concat_axis=0, tiled=True)  6.66 us
    all_to_all x1, waiting for transfers between devices, shards(): lax.all_to_all(spectrum, ('lat', 'lon'), split_axis=0, concat_axis=0, til...  4.89 us
    ppermute x4, starting transfers between devices, shards(): pieces.append(lax.ppermute(piece, ('lat', 'lon'), pairs))  3.88 us
  transfers between devices with their start and end apart: 6, of which 6 were waited for; matrix products, arithmetic and copies ran while one was open for 0% of the time, Pallas kernels for 19%

profile of v4, /device:TPU:1, one launch (start us, length us, event | category | flops | bytes accessed | tf_op | source)
XLA Modules:
  0.0 102.5 jit_solution(12352480852099562285)
XLA Ops:
  0.6 0.0 copy-start.1
  0.6 0.0 copy-start.2
  0.7 2.1 %pack.1 = (f32[4,64,640]{2,1,0:T(8,128)}, f32[2,8,128]{2,1,0:T(8,128)S(1)}, f32[8,640]{1,0:T(8,128)S(1)}) custom-call(s32[1]{0:T(128)} %bitcast.rank_ref, f32[1280]{0:T(1024)} %constant.32.clone.logs_hbm, f32[8,640]{1,0:T(8,128)} %constant.33.clone.lat_hbm, f32[2,40,640]{2,1,0:T(8,128)} %vort_hbm.1, f32[2,40,640]{2,1,0:T(8,128)} %div_hbm.1, ...), custom_call_target="tpu_custom_call" | custom-call | flops 1048576 | bytes 2097152 | tf_op jit(solution)/shard_map/pack/pallas_call | solution.py:696
  2.8 6.7 %all-to-all-start = ((f32[4,64,640]{2,1,0:T(8,128)}), f32[4,64,640]{2,1,0:T(8,128)S(1)}, u32[]{:S(2)}, u32[]{:S(2)}) async-start(f32[4,64,640]{2,1,0:T(8,128)} %get-tuple-element.17), calls=%async_computation | async-start | bytes 1310720 | tf_op jit(solution)/shard_map/all_to_all | solution.py:707
  9.4 9.2 %table.2 = (bf16[10,2,2,256,640]{4,3,2,1,0:T(8,128)(2,1)}, f32[3,8,640]{2,1,0:T(8,128)S(1)}) custom-call(s32[1]{0:T(128)} %bitcast.rank_ref, f32[2,8,128]{2,1,0:T(8,128)S(1)} %get-tuple-element.18.logs_ref, f32[8,640]{1,0:T(8,128)S(1)} %get-tuple-element.19.lat_ref, f32[3,8,640]{2,1,0:T(8,128)S(1)} %broadcast_in_dim.3.before_ref), custom_call_target="tpu_custom_call" | custom-call | flops 4294967296 | bytes 13631488 | tf_op jit(solution)/shard_map/table/pallas_call | solution.py:668
  18.7 0.0 copy-start.4
  18.7 0.0 copy-start.5
  18.7 0.0 copy-start.6
  18.7 0.0 copy-start.7
  18.7 1.6 %all-to-all-done.in_ref = f32[4,64,640]{2,1,0:T(8,128)S(1)} async-done(((f32[4,64,640]{2,1,0:T(8,128)}), f32[4,64,640]{2,1,0:T(8,128)S(1)}, u32[]{:S(2)}, u32[]{:S(2)}) %all-to-all-start) | async-done | bytes 655392 | tf_op jit(solution)/shard_map/all_to_all | solution.py:707
  20.3 0.0 copy-done.1
  20.3 0.0 copy-done.2
  20.3 1.3 %forward.1 = f32[128,1280]{1,0:T(8,128)S(1)} custom-call(f32[4,64,640]{2,1,0:T(8,128)S(1)} %all-to-all-done.in_ref, f32[40,128]{1,0:T(8,128)S(1)} %copy-done.1, bf16[128,256]{1,0:T(8,128)(2,1)S(1)} %copy-done.2), custom_call_target="tpu_custom_call" | custom-call | flops 268435456 | bytes 2097152 | tf_op jit(solution)/shard_map/forward/pallas_call | solution.py:709
  21.6 1.5 %copy.16 = f32[128,1,1280]{2,1,0:T(1,128)} copy(f32[128,1,1280]{2,0,1:T(8,128)S(1)} %bitcast.10) | data formatting | bytes 1310720 | tf_op jit(solution)/shard_map/all_to_all | solution.py:720
  23.1 8.1 %all-to-all-start.1 = ((f32[128,1,1280]{2,1,0:T(1,128)}), f32[128,1,1280]{2,1,0:T(1,128)S(1)}, u32[]{:S(2)}, u32[]{:S(2)}) async-start(f32[128,1,1280]{2,1,0:T(1,128)} %copy.16), calls=%async_computation.1 | async-start | bytes 1310720 | tf_op jit(solution)/shard_map/all_to_all | solution.py:720
  31.3 9.8 %table.3 = (bf16[10,2,2,256,640]{4,3,2,1,0:T(8,128)(2,1)}, f32[3,8,640]{2,1,0:T(8,128)}) custom-call(s32[1]{0:T(128)} %bitcast.rank_ref, f32[2,8,128]{2,1,0:T(8,128)S(1)} %get-tuple-element.18.logs_ref, f32[8,640]{1,0:T(8,128)S(1)} %get-tuple-element.19.lat_ref, f32[3,8,640]{2,1,0:T(8,128)S(1)} %get-tuple-element.25.before_ref), custom_call_target="tpu_custom_call" | custom-call | flops 4294967296 | bytes 13631488 | tf_op jit(solution)/shard_map/table/pallas_call | solution.py:668
  41.1 4.9 %all-to-all-done.1 = f32[128,1,1280]{2,1,0:T(1,128)S(1)} async-done(((f32[128,1,1280]{2,1,0:T(1,128)}), f32[128,1,1280]{2,1,0:T(1,128)S(1)}, u32[]{:S(2)}, u32[]{:S(2)}) %all-to-all-start.1) | async-done | bytes 655392 | tf_op jit(solution)/shard_map/all_to_all | solution.py:720
  46.0 0.0 copy-done.4
  46.0 0.0 copy-done.5
  46.0 0.0 copy-done.6
  46.0 0.0 copy-done.7
  46.1 0.0 copy-start
  46.1 0.0 copy-start.3
  46.1 20.7 %legendre.1 = f32[128,1280]{1,0:T(8,128)S(1)} custom-call(s32[1]{0:T(128)} %bitcast.rank_ref, f32[2]{0:T(128)S(1)} %copy-done.4, f32[128,1280]{1,0:T(8,128)S(1)} %bitcast.11, f32[8,640]{1,0:T(8,128)S(1)} %get-tuple-element.19.lat_ref, bf16[240,256]{1,0:T(8,128)(2,1)S(1)} %copy-done.7, bf16[512,256]{1,0:T(8,128)(2,1)S(1)} %copy-done.5, ...), custom_call_target="tpu_custom_call" | custom-call | flops 8589934592 | bytes 2097152 | tf_op jit(solution)/shard_map/legendre/pallas_call | solution.py:721
  66.7 0.7 copy.17
  67.4 19.4 %all_to_all.27 = f32[128,1,1280]{2,1,0:T(1,128)S(1)} all-to-all(f32[128,1,1280]{2,1,0:T(1,128)S(1)} %copy.17), channel_id=1, replica_groups=mesh['lat'=32,'lon'=4] {'lat','lon'}, dimensions={0} | all-to-all | bytes 1310720 | tf_op jit(solution)/shard_map/all_to_all | solution.py:748
  86.9 0.0 copy-done
  86.9 0.0 copy-done.3
  86.9 2.9 %inverse.1 = (f32[64,640]{1,0:T(8,128)S(1)}, f32[64,640]{1,0:T(8,128)S(1)}, f32[64,640]{1,0:T(8,128)S(1)}, f32[64,640]{1,0:T(8,128)S(1)}) custom-call(s32[1]{0:T(128)} %bitcast.rank_ref, f32[128,1280]{1,0:T(8,128)S(1)} %bitcast.9, bf16[160,128]{1,0:T(8,128)(2,1)S(1)} %copy-done.3, f32[40,128]{1,0:T(8,128)S(1)} %copy-done.1, bf16[1024,256]{1,0:T(8,128)(2,1)S(1)} %copy-done), custom_call_target="tpu_custom_call" | custom-call | flops 268435456 | bytes 2097152 | tf_op jit(solution)/shard_map/inverse/pallas_call | solution.py:749
  89.8 0.6 collective-permute-start
  90.4 1.9 %collective-permute-start.1 = (f32[64,640]{1,0:T(8,128)S(1)}, f32[64,640]{1,0:T(8,128)S(1)}, u32[]{:S(2)}, u32[]{:S(2)}) collective-permute-start(f32[64,640]{1,0:T(8,128)S(1)} %get-tuple-element.28), channel_id=1, source_target_pairs={{0,65},{1,66},{2,67},{3,64},{4,69},{5,70},{6,71},{7,68},{8,73},{9,... | collective-permute-start | bytes 491528 | tf_op jit(solution)/shard_map/ppermute | solution.py:771
  92.3 1.4 %collective-permute-start.2 = (f32[64,640]{1,0:T(8,128)S(1)}, f32[64,640]{1,0:T(8,128)S(1)}, u32[]{:S(2)}, u32[]{:S(2)}) collective-permute-start(f32[64,640]{1,0:T(8,128)S(1)} %get-tuple-element.29), channel_id=1, source_target_pairs={{0,66},{1,67},{2,64},{3,65},{4,70},{5,71},{6,68},{7,69},{8,74},{9,... | collective-permute-start | bytes 491528 | tf_op jit(solution)/shard_map/ppermute | solution.py:771
  93.6 0.0 collective-permute-start.3
  93.6 1.6 %collective-permute-done.in0_ref = f32[64,640]{1,0:T(8,128)S(1)} collective-permute-done((f32[64,640]{1,0:T(8,128)S(1)}, f32[64,640]{1,0:T(8,128)S(1)}, u32[]{:S(2)}, u32[]{:S(2)}) %collective-permute-start) | collective-permute-done | bytes 163872 | tf_op jit(solution)/shard_map/ppermute | solution.py:771
  95.2 4.3 %collective-permute-done.1.in1_ref = f32[64,640]{1,0:T(8,128)S(1)} collective-permute-done((f32[64,640]{1,0:T(8,128)S(1)}, f32[64,640]{1,0:T(8,128)S(1)}, u32[]{:S(2)}, u32[]{:S(2)}) %collective-permute-start.1) | collective-permute-done | bytes 163872 | tf_op jit(solution)/shard_map/ppermute | solution.py:771
  99.6 0.8 collective-permute-done.2.in2_ref
  100.4 1.2 %collective-permute-done.3.in3_ref = f32[64,640]{1,0:T(8,128)S(1)} collective-permute-done((f32[64,640]{1,0:T(8,128)S(1)}, f32[64,640]{1,0:T(8,128)S(1)}, u32[]{:S(2)}, u32[]{:S(2)}) %collective-permute-start.3) | collective-permute-done | bytes 163872 | tf_op jit(solution)/shard_map/ppermute | solution.py:771
  101.6 0.9 unpack.1
  (3 shorter events, 0.1 us)
Async XLA Ops:
  0.6 19.7 %copy-start.1 = (f32[40,128]{1,0:T(8,128)S(1)}, f32[40,128]{1,0:T(8,128)}, u32[]{:S(2)}) copy-start(f32[40,128]{1,0:T(8,128)} %constant.31.clone.twiddle_ref) | copy-start | bytes 61444
  0.6 19.7 %copy-start.2 = (bf16[128,256]{1,0:T(8,128)(2,1)S(1)}, bf16[128,256]{1,0:T(8,128)(2,1)}, u32[]{:S(2)}) copy-start(bf16[128,256]{1,0:T(8,128)(2,1)} %constant.34.clone.table_ref) | copy-start | bytes 196612
  2.8 17.5 %all-to-all-start = ((f32[4,64,640]{2,1,0:T(8,128)}), f32[4,64,640]{2,1,0:T(8,128)S(1)}, u32[]{:S(2)}, u32[]{:S(2)}) async-start(f32[4,64,640]{2,1,0:T(8,128)} %get-tuple-element.17), calls=%async_computation | async-start | bytes 1310720 | tf_op jit(solution)/shard_map/all_to_all | solution.py:707
  18.7 27.3 %copy-start.4 = (f32[2]{0:T(128)S(1)}, f32[2]{0:T(128)}, u32[]{:S(2)}) copy-start(f32[2]{0:T(128)} %geo_ref.1) | copy-start | bytes 28
  18.7 27.3 %copy-start.5 = (bf16[512,256]{1,0:T(8,128)(2,1)S(1)}, bf16[512,256]{1,0:T(8,128)(2,1)}, u32[]{:S(2)}) copy-start(bf16[512,256]{1,0:T(8,128)(2,1)} %constant.36.clone.fold_ref) | copy-start | bytes 786436
  18.7 27.3 %copy-start.6 = (bf16[256,256]{1,0:T(8,128)(2,1)S(1)}, bf16[256,256]{1,0:T(8,128)(2,1)}, u32[]{:S(2)}) copy-start(bf16[256,256]{1,0:T(8,128)(2,1)} %constant.37.clone.unfold_ref) | copy-start | bytes 393220
  18.7 27.3 %copy-start.7 = (bf16[240,256]{1,0:T(8,128)(2,1)S(1)}, bf16[240,256]{1,0:T(8,128)(2,1)}, u32[]{:S(2)}) copy-start(bf16[240,256]{1,0:T(8,128)(2,1)} %constant.35.clone.gather_ref) | copy-start | bytes 368644
  23.1 22.8 %all-to-all-start.1 = ((f32[128,1,1280]{2,1,0:T(1,128)}), f32[128,1,1280]{2,1,0:T(1,128)S(1)}, u32[]{:S(2)}, u32[]{:S(2)}) async-start(f32[128,1,1280]{2,1,0:T(1,128)} %copy.16), calls=%async_computation.1 | async-start | bytes 1310720 | tf_op jit(solution)/shard_map/all_to_all | solution.py:720
  46.1 40.8 %copy-start = (bf16[1024,256]{1,0:T(8,128)(2,1)S(1)}, bf16[1024,256]{1,0:T(8,128)(2,1)}, u32[]{:S(2)}) copy-start(bf16[1024,256]{1,0:T(8,128)(2,1)} %constant.39.clone.table_ref) | copy-start | bytes 1572868
  46.1 40.8 %copy-start.3 = (bf16[160,128]{1,0:T(8,128)(2,1)S(1)}, bf16[160,128]{1,0:T(8,128)(2,1)}, u32[]{:S(2)}) copy-start(bf16[160,128]{1,0:T(8,128)(2,1)} %constant.38.clone.scatter_ref) | copy-start | bytes 122884
  89.8 5.5 %collective-permute-start = (f32[64,640]{1,0:T(8,128)S(1)}, f32[64,640]{1,0:T(8,128)S(1)}, u32[]{:S(2)}, u32[]{:S(2)}) collective-permute-start(f32[64,640]{1,0:T(8,128)S(1)} %get-tuple-element.27), channel_id=1, source_target_pairs={{0,64},{1,65},{2,66},{3,67},{4,68},{5,69},{6,70},{7,71},{8,72},{9,... | collective-permute-start | bytes 491528 | tf_op jit(solution)/shard_map/ppermute | solution.py:771
  90.4 9.2 %collective-permute-start.1 = (f32[64,640]{1,0:T(8,128)S(1)}, f32[64,640]{1,0:T(8,128)S(1)}, u32[]{:S(2)}, u32[]{:S(2)}) collective-permute-start(f32[64,640]{1,0:T(8,128)S(1)} %get-tuple-element.28), channel_id=1, source_target_pairs={{0,65},{1,66},{2,67},{3,64},{4,69},{5,70},{6,71},{7,68},{8,73},{9,... | collective-permute-start | bytes 491528 | tf_op jit(solution)/shard_map/ppermute | solution.py:771
  92.3 8.1 %collective-permute-start.2 = (f32[64,640]{1,0:T(8,128)S(1)}, f32[64,640]{1,0:T(8,128)S(1)}, u32[]{:S(2)}, u32[]{:S(2)}) collective-permute-start(f32[64,640]{1,0:T(8,128)S(1)} %get-tuple-element.29), channel_id=1, source_target_pairs={{0,66},{1,67},{2,64},{3,65},{4,70},{5,71},{6,68},{7,69},{8,74},{9,... | collective-permute-start | bytes 491528 | tf_op jit(solution)/shard_map/ppermute | solution.py:771
  93.6 8.0 %collective-permute-start.3 = (f32[64,640]{1,0:T(8,128)S(1)}, f32[64,640]{1,0:T(8,128)S(1)}, u32[]{:S(2)}, u32[]{:S(2)}) collective-permute-start(f32[64,640]{1,0:T(8,128)S(1)} %get-tuple-element.30), channel_id=1, source_target_pairs={{0,67},{1,64},{2,65},{3,66},{4,71},{5,68},{6,69},{7,70},{8,75},{9,... | collective-permute-start | bytes 491528 | tf_op jit(solution)/shard_map/ppermute | solution.py:771

commit v5 on v4

--- a/solution.py
+++ b/solution.py
@@ -75,12 +75,12 @@
 def fold_matrix():
     out = np.zeros((4, 128, 2, 128), np.float32)
     for src in range(64):
-        out[0, src, :, src] = 1.0
-        out[1, src, :, 64 + src] = 1.0
-        out[2, 127 - src, 0, src] = 1.0
-        out[2, 127 - src, 1, src] = -1.0
-        out[3, 127 - src, 0, 64 + src] = 1.0
-        out[3, 127 - src, 1, 64 + src] = -1.0
+        out[0, src ^ 64, :, src] = 1.0
+        out[1, src ^ 64, :, 64 + src] = 1.0
+        out[2, (127 - src) ^ 64, 0, src] = 1.0
+        out[2, (127 - src) ^ 64, 1, src] = -1.0
+        out[3, (127 - src) ^ 64, 0, 64 + src] = 1.0
+        out[3, (127 - src) ^ 64, 1, 64 + src] = -1.0
     return out.reshape(512, 256).astype(ml_dtypes.bfloat16)
 
 
@@ -154,7 +154,10 @@
     vort_hbm,
     div_hbm,
     height_hbm,
-    out_ref,
+    out0_ref,
+    out1_ref,
+    out2_ref,
+    out3_ref,
     start_ref,
     lat_ref,
     vort_ref,
@@ -177,15 +180,23 @@
     ]
     for copy in copies:
         copy.start()
-    for b in range(4):
-        out_ref[b, pl.ds(60, 4), :] = jnp.zeros((4, 640), F32)
-    for f, ref in enumerate((vort_ref, div_ref, height_ref)):
-        copies[f].wait()
+    pieces = (out0_ref, out1_ref, out2_ref, out3_ref)
+    for piece_ref in pieces:
+        piece_ref[pl.ds(60, 4), :] = jnp.zeros((4, 640), F32)
+    for copy in copies:
+        copy.wait()
+
+    def place(lon):
         for b in range(4):
-            for lev in range(2):
-                out_ref[b, pl.ds((2 * f + lev) * 10, 10), :] = ref[lev, pl.ds(10 * b, 10), :]
-    copies[3].wait()
-    copies[4].wait()
+            for f, ref in enumerate((vort_ref, div_ref, height_ref)):
+                for lev in range(2):
+                    pieces[(b - lon) % 4][pl.ds((2 * f + lev) * 10, 10), :] = ref[
+                        lev, pl.ds(10 * b, 10), :
+                    ]
+
+    for lon in range(4):
+        pl.when(rank_ref[0] % 4 == lon)(functools.partial(place, lon))
+
     rank = rank_ref[0]
     first = (rank % 32) * 20 + (rank // 32) * 5
     sub = lax.broadcasted_iota(jnp.int32, (8, LANES), 0)
@@ -214,7 +225,21 @@
         pl.when(rank_ref[0] % 4 == lon)(functools.partial(place, lon))
 
 
-def forward_kernel(in_ref, twiddle_ref, table_ref, out_ref, z_ref):
+def forward_kernel(
+    rank_ref,
+    in0_ref,
+    in1_ref,
+    in2_ref,
+    in3_ref,
+    twiddle_ref,
+    table_ref,
+    out_ref,
+    z_ref,
+    in_ref,
+):
+    for shift, piece_ref in enumerate((in0_ref, in1_ref, in2_ref, in3_ref)):
+        in_ref[(rank_ref[0] + 4 - shift) % 4] = piece_ref[...]
+
     @pl.loop(0, 8)
     def _(group):
         rows = pl.ds(pl.multiple_of(group * 8, 8), 8)
@@ -688,14 +713,28 @@
     )(rank, logs, lat, before)
 
 
+def exchange(pieces):
+    n_lat = lax.axis_size("lat")
+    n_lon = lax.axis_size("lon")
+    moved = []
+    for shift, piece in enumerate(pieces):
+        pairs = [
+            (lat_at * n_lon + lon_at, (lat_at ^ 16) * n_lon + (lon_at + shift) % n_lon)
+            for lat_at in range(n_lat)
+            for lon_at in range(n_lon)
+        ]
+        moved.append(lax.ppermute(piece, ("lat", "lon"), pairs))
+    return tuple(moved)
+
+
 def shards(vorticity, divergence, height, mean_geopot):
     rank = lax.axis_index("lat") * lax.axis_size("lon") + lax.axis_index("lon")
     rank = rank.astype(jnp.int32).reshape(1)
     twiddle = jnp.asarray(twiddles())
     sources = (jnp.asarray(sector_logs()), jnp.asarray(latitude_rows()), vorticity, divergence, height)
-    packed, logs, lat = call(
+    *packed, logs, lat = call(
         pack_kernel,
-        [(4, 64, 640), (2, 8, LANES), (8, 640)],
+        [(64, 640)] * 4 + [(2, 8, LANES), (8, 640)],
         [SMEM] + [HBM] * 5,
         [pltpu.VMEM((2, 40, 640), F32) for _ in range(3)]
         + [pltpu.SMEM((MMAX,), F32), pltpu.SemaphoreType.DMA((5,))],
@@ -704,17 +743,17 @@
         "pack",
     )(rank, *(pltpu.with_memory_space_constraint(x, pltpu.HBM) for x in sources))
     early, state = table_call(0, rank, logs, lat, jnp.zeros((3, 8, 640), F32))
-    sectors = lax.all_to_all(packed, "lon", split_axis=0, concat_axis=0, tiled=True)
+    sectors = exchange(packed)
     sectors, state = lax.optimization_barrier((sectors, state))
     spectrum = call(
         forward_kernel,
         [(128, 1280)],
-        [VMEM] * 3,
-        [pltpu.VMEM((20, 64, 256), F32)],
+        [SMEM] + [VMEM] * 6,
+        [pltpu.VMEM((20, 64, 256), F32), pltpu.VMEM((4, 64, 640), F32)],
         16,
         1 << 28,
         "forward",
-    )(sectors, twiddle, jnp.asarray(forward_matrix()))
+    )(rank, *sectors, twiddle, jnp.asarray(forward_matrix()))
     spectrum, state = lax.optimization_barrier((spectrum, state))
     late, _ = table_call(1, rank, logs, lat, state)
     columns = lax.all_to_all(spectrum, ("lat", "lon"), split_axis=0, concat_axis=0, tiled=True)
@@ -759,16 +798,7 @@
         1 << 28,
         "inverse",
     )(rank, gathered, jnp.asarray(scatter_matrix()), twiddle, jnp.asarray(inverse_matrix()))
-    n_lat = lax.axis_size("lat")
-    n_lon = lax.axis_size("lon")
-    pieces = []
-    for shift, piece in enumerate(result):
-        pairs = [
-            (lat_at * n_lon + lon_at, (lat_at ^ 16) * n_lon + (lon_at + shift) % n_lon)
-            for lat_at in range(n_lat)
-            for lon_at in range(n_lon)
-        ]
-        pieces.append(lax.ppermute(piece, ("lat", "lon"), pairs))
+    pieces = exchange(result)
     return call(unpack_kernel, [(2, 40, 640)] * 3, [SMEM] + [VMEM] * 4, [], 8, 1 << 20, "unpack")(
         rank, *pieces
     )

time: 103 us -> 101 us (0.981)
  waiting for transfers between devices: 14.4 us -> 12.9 us
    ppermute x4 -> x8, starting transfers between devices: 3.88 us -> 10.5 us  [exchange(): moved.append(lax.ppermute(piece, ('lat', 'lon'), pairs))]
    all_to_all x1 -> x0, starting transfers between devices: 6.66 us -> none  [shards(): lax.all_to_all(packed, 'lon', split_axis=0, concat_axis=0, tiled=True)]
    all_to_all x1 -> x0, waiting for transfers between devices: 1.58 us -> none  [shards(): lax.all_to_all(packed, 'lon', split_axis=0, concat_axis=0, tiled=True)]
    ppermute x4 -> x8, waiting for transfers between devices: 7.96 us -> 7.98 us  [exchange(): moved.append(lax.ppermute(piece, ('lat', 'lon'), pairs))]
  transfers between devices with their start and end apart: 6 -> 9, of which waited for: 6 -> 5; matrix products, arithmetic and copies ran while one was open for 0% -> 0% of each run, Pallas kernels for 19% -> 19%
where the time goes in v5:
time: 101 us
  Pallas kernels  46.2 us (46%)
  blocking collectives  19.4 us (19%)
  starting transfers between devices  19.2 us (19%)
  waiting for transfers between devices  12.9 us (13%)
  local copies, waits for them, and re-layouts  2.34 us (2%)
    pallas_call x1, Pallas kernels, shards(): call(legendre_kernel, [(128, 1280)], [SMEM] * 2 + [VMEM] * 5 + [HBM] * 2,...  20.7 us
    all_to_all x1, blocking collectives, shards(): lax.all_to_all(synthesis, ('lat', 'lon'), split_axis=0, concat_axis=0, ti...  19.4 us
    pallas_call x2, Pallas kernels, table_call(): pl.pallas_call(functools.partial(table_kernel, phase), grid=(HALF,), out_...  19 us
    ppermute x8, starting transfers between devices, exchange(): moved.append(lax.ppermute(piece, ('lat', 'lon'), pairs))  10.5 us
    all_to_all x1, starting transfers between devices, shards(): lax.all_to_all(spectrum, ('lat', 'lon'), split_axis=0, concat_axis=0, til...  8.68 us
    ppermute x8, waiting for transfers between devices, exchange(): moved.append(lax.ppermute(piece, ('lat', 'lon'), pairs))  7.98 us
    all_to_all x1, waiting for transfers between devices, shards(): lax.all_to_all(spectrum, ('lat', 'lon'), split_axis=0, concat_axis=0, til...  4.89 us
    pallas_call x1, Pallas kernels, shards(): call(inverse_kernel, [(64, 640)] * 4, [SMEM] + [VMEM] * 4, [pltpu.VMEM((4...  2.87 us
  transfers between devices with their start and end apart: 9, of which 5 were waited for; matrix products, arithmetic and copies ran while one was open for 0% of the time, Pallas kernels for 19%

profile of v5, /device:TPU:1, one launch (start us, length us, event | category | flops | bytes accessed | tf_op | source)
XLA Modules:
  0.0 100.9 jit_solution(12788974260432509245)
XLA Ops:
  0.6 0.0 copy-start.1
  0.6 0.0 copy-start.2
  0.7 1.4 %pack.1 = (f32[64,640]{1,0:T(8,128)S(1)}, f32[64,640]{1,0:T(8,128)S(1)}, f32[64,640]{1,0:T(8,128)S(1)}, f32[64,640]{1,0:T(8,128)S(1)}, f32[2,8,128]{2,1,0:T(8,128)S(1)}, /*index=5*/f32[8,640]{1,0:T(8,128)S(1)}) custom-call(s32[1]{0:T(128)} %bitcast.rank_ref, f32[1280]{0:T(1024)} %constant.32.clone.logs_hbm, f32[8,640]{1,0:T(8,128)} %constant.33.clone.lat_hbm, ...), custom_call_target="tpu_custom_call" | custom-call | flops 1048576 | bytes 2097152 | tf_op jit(solution)/shard_map/pack/pallas_call | solution.py:735
  2.0 2.5 %collective-permute-start = (f32[64,640]{1,0:T(8,128)S(1)}, f32[64,640]{1,0:T(8,128)S(1)}, u32[]{:S(2)}, u32[]{:S(2)}) collective-permute-start(f32[64,640]{1,0:T(8,128)S(1)} %get-tuple-element.23), channel_id=1, source_target_pairs={{0,64},{1,65},{2,66},{3,67},{4,68},{5,69},{6,70},{7,71},{8,72},{9,... | collective-permute-start | bytes 491528 | tf_op jit(solution)/shard_map/ppermute | solution.py:726
  4.6 3.1 %collective-permute-start.1 = (f32[64,640]{1,0:T(8,128)S(1)}, f32[64,640]{1,0:T(8,128)S(1)}, u32[]{:S(2)}, u32[]{:S(2)}) collective-permute-start(f32[64,640]{1,0:T(8,128)S(1)} %get-tuple-element.24), channel_id=1, source_target_pairs={{0,65},{1,66},{2,67},{3,64},{4,69},{5,70},{6,71},{7,68},{8,73},{9,... | collective-permute-start | bytes 491528 | tf_op jit(solution)/shard_map/ppermute | solution.py:726
  7.7 0.4 collective-permute-start.2
  8.1 0.6 collective-permute-start.3
  8.7 9.2 %table.2 = (bf16[10,2,2,256,640]{4,3,2,1,0:T(8,128)(2,1)}, f32[3,8,640]{2,1,0:T(8,128)S(1)}) custom-call(s32[1]{0:T(128)} %bitcast.rank_ref, f32[2,8,128]{2,1,0:T(8,128)S(1)} %get-tuple-element.27.logs_ref, f32[8,640]{1,0:T(8,128)S(1)} %get-tuple-element.28.lat_ref, f32[3,8,640]{2,1,0:T(8,128)S(1)} %broadcast_in_dim.3.before_ref), custom_call_target="tpu_custom_call" | custom-call | flops 4294967296 | bytes 13631488 | tf_op jit(solution)/shard_map/table/pallas_call | solution.py:693
  18.0 0.0 copy-start.4
  18.0 0.0 copy-start.5
  18.0 0.0 copy-start.6
  18.0 0.0 copy-start.7
  18.0 0.0 collective-permute-done.in0_ref
  18.0 0.0 collective-permute-done.1.in1_ref
  18.0 0.0 collective-permute-done.2.in2_ref
  18.0 0.0 collective-permute-done.3.in3_ref
  18.1 0.0 copy-done.1
  18.1 0.0 copy-done.2
  18.1 1.3 %forward.1 = f32[128,1280]{1,0:T(8,128)S(1)} custom-call(s32[1]{0:T(128)} %bitcast.rank_ref, f32[64,640]{1,0:T(8,128)S(1)} %collective-permute-done.in0_ref, f32[64,640]{1,0:T(8,128)S(1)} %collective-permute-done.1.in1_ref, f32[64,640]{1,0:T(8,128)S(1)} %collective-permute-done.2.in2_ref, f32[64,640]{1,0:T(8,128)S(1)} %collective-permute-done.3.in3_ref, ...), custom_call_target="tpu_custom_call" | custom-call | flops 268435456 | bytes 2097152 | tf_op jit(solution)/shard_map/forward/pallas_call | solution.py:748
  19.4 1.5 %copy.16 = f32[128,1,1280]{2,1,0:T(1,128)} copy(f32[128,1,1280]{2,0,1:T(8,128)S(1)} %bitcast.10) | data formatting | bytes 1310720 | tf_op jit(solution)/shard_map/all_to_all | solution.py:759
  20.9 8.7 %all-to-all-start = ((f32[128,1,1280]{2,1,0:T(1,128)}), f32[128,1,1280]{2,1,0:T(1,128)S(1)}, u32[]{:S(2)}, u32[]{:S(2)}) async-start(f32[128,1,1280]{2,1,0:T(1,128)} %copy.16), calls=%async_computation | async-start | bytes 1310720 | tf_op jit(solution)/shard_map/all_to_all | solution.py:759
  29.6 9.8 %table.3 = (bf16[10,2,2,256,640]{4,3,2,1,0:T(8,128)(2,1)}, f32[3,8,640]{2,1,0:T(8,128)}) custom-call(s32[1]{0:T(128)} %bitcast.rank_ref, f32[2,8,128]{2,1,0:T(8,128)S(1)} %get-tuple-element.27.logs_ref, f32[8,640]{1,0:T(8,128)S(1)} %get-tuple-element.28.lat_ref, f32[3,8,640]{2,1,0:T(8,128)S(1)} %get-tuple-element.37.before_ref), custom_call_target="tpu_custom_call" | custom-call | flops 4294967296 | bytes 13631488 | tf_op jit(solution)/shard_map/table/pallas_call | solution.py:693
  39.5 4.9 %all-to-all-done = f32[128,1,1280]{2,1,0:T(1,128)S(1)} async-done(((f32[128,1,1280]{2,1,0:T(1,128)}), f32[128,1,1280]{2,1,0:T(1,128)S(1)}, u32[]{:S(2)}, u32[]{:S(2)}) %all-to-all-start) | async-done | bytes 655392 | tf_op jit(solution)/shard_map/all_to_all | solution.py:759
  44.4 0.0 copy-done.4
  44.4 0.0 copy-done.5
  44.4 0.0 copy-done.6
  44.4 0.0 copy-done.7
  44.4 0.0 copy-start
  44.4 0.0 copy-start.3
  44.5 20.7 %legendre.1 = f32[128,1280]{1,0:T(8,128)S(1)} custom-call(s32[1]{0:T(128)} %bitcast.rank_ref, f32[2]{0:T(128)S(1)} %copy-done.4, f32[128,1280]{1,0:T(8,128)S(1)} %bitcast.11, f32[8,640]{1,0:T(8,128)S(1)} %get-tuple-element.28.lat_ref, bf16[240,256]{1,0:T(8,128)(2,1)S(1)} %copy-done.7, bf16[512,256]{1,0:T(8,128)(2,1)S(1)} %copy-done.5, ...), custom_call_target="tpu_custom_call" | custom-call | flops 8589934592 | bytes 2097152 | tf_op jit(solution)/shard_map/legendre/pallas_call | solution.py:760
  65.1 0.7 copy.17
  65.8 19.4 %all_to_all.22 = f32[128,1,1280]{2,1,0:T(1,128)S(1)} all-to-all(f32[128,1,1280]{2,1,0:T(1,128)S(1)} %copy.17), channel_id=1, replica_groups=mesh['lat'=32,'lon'=4] {'lat','lon'}, dimensions={0} | all-to-all | bytes 1310720 | tf_op jit(solution)/shard_map/all_to_all | solution.py:787
  85.3 0.0 copy-done
  85.3 0.0 copy-done.3
  85.3 2.9 %inverse.1 = (f32[64,640]{1,0:T(8,128)S(1)}, f32[64,640]{1,0:T(8,128)S(1)}, f32[64,640]{1,0:T(8,128)S(1)}, f32[64,640]{1,0:T(8,128)S(1)}) custom-call(s32[1]{0:T(128)} %bitcast.rank_ref, f32[128,1280]{1,0:T(8,128)S(1)} %bitcast.9, bf16[160,128]{1,0:T(8,128)(2,1)S(1)} %copy-done.3, f32[40,128]{1,0:T(8,128)S(1)} %copy-done.1, bf16[1024,256]{1,0:T(8,128)(2,1)S(1)} %copy-done), custom_call_target="tpu_custom_call" | custom-call | flops 268435456 | bytes 2097152 | tf_op jit(solution)/shard_map/inverse/pallas_call | solution.py:788
  88.1 0.6 collective-permute-start.4
  88.8 1.9 %collective-permute-start.5 = (f32[64,640]{1,0:T(8,128)S(1)}, f32[64,640]{1,0:T(8,128)S(1)}, u32[]{:S(2)}, u32[]{:S(2)}) collective-permute-start(f32[64,640]{1,0:T(8,128)S(1)} %get-tuple-element.40), channel_id=1, source_target_pairs={{0,65},{1,66},{2,67},{3,64},{4,69},{5,70},{6,71},{7,68},{8,73},{9,... | collective-permute-start | bytes 491528 | tf_op jit(solution)/shard_map/ppermute | solution.py:726
  90.7 1.4 %collective-permute-start.6 = (f32[64,640]{1,0:T(8,128)S(1)}, f32[64,640]{1,0:T(8,128)S(1)}, u32[]{:S(2)}, u32[]{:S(2)}) collective-permute-start(f32[64,640]{1,0:T(8,128)S(1)} %get-tuple-element.41), channel_id=1, source_target_pairs={{0,66},{1,67},{2,64},{3,65},{4,70},{5,71},{6,68},{7,69},{8,74},{9,... | collective-permute-start | bytes 491528 | tf_op jit(solution)/shard_map/ppermute | solution.py:726
  92.0 0.0 collective-permute-start.7
  92.0 1.6 %collective-permute-done.4.in0_ref = f32[64,640]{1,0:T(8,128)S(1)} collective-permute-done((f32[64,640]{1,0:T(8,128)S(1)}, f32[64,640]{1,0:T(8,128)S(1)}, u32[]{:S(2)}, u32[]{:S(2)}) %collective-permute-start.4) | collective-permute-done | bytes 163872 | tf_op jit(solution)/shard_map/ppermute | solution.py:726
  93.6 4.3 %collective-permute-done.5.in1_ref = f32[64,640]{1,0:T(8,128)S(1)} collective-permute-done((f32[64,640]{1,0:T(8,128)S(1)}, f32[64,640]{1,0:T(8,128)S(1)}, u32[]{:S(2)}, u32[]{:S(2)}) %collective-permute-start.5) | collective-permute-done | bytes 163872 | tf_op jit(solution)/shard_map/ppermute | solution.py:726
  98.0 0.8 collective-permute-done.6.in2_ref
  98.7 1.2 %collective-permute-done.7.in3_ref = f32[64,640]{1,0:T(8,128)S(1)} collective-permute-done((f32[64,640]{1,0:T(8,128)S(1)}, f32[64,640]{1,0:T(8,128)S(1)}, u32[]{:S(2)}, u32[]{:S(2)}) %collective-permute-start.7) | collective-permute-done | bytes 163872 | tf_op jit(solution)/shard_map/ppermute | solution.py:726
  100.0 0.9 unpack.1
  (3 shorter events, 0.1 us)
Async XLA Ops:
  0.6 17.4 %copy-start.1 = (f32[40,128]{1,0:T(8,128)S(1)}, f32[40,128]{1,0:T(8,128)}, u32[]{:S(2)}) copy-start(f32[40,128]{1,0:T(8,128)} %constant.31.clone.twiddle_ref) | copy-start | bytes 61444
  0.6 17.4 %copy-start.2 = (bf16[128,256]{1,0:T(8,128)(2,1)S(1)}, bf16[128,256]{1,0:T(8,128)(2,1)}, u32[]{:S(2)}) copy-start(bf16[128,256]{1,0:T(8,128)(2,1)} %constant.34.clone.table_ref) | copy-start | bytes 196612
  2.0 16.0 %collective-permute-start = (f32[64,640]{1,0:T(8,128)S(1)}, f32[64,640]{1,0:T(8,128)S(1)}, u32[]{:S(2)}, u32[]{:S(2)}) collective-permute-start(f32[64,640]{1,0:T(8,128)S(1)} %get-tuple-element.23), channel_id=1, source_target_pairs={{0,64},{1,65},{2,66},{3,67},{4,68},{5,69},{6,70},{7,71},{8,72},{9,... | collective-permute-start | bytes 491528 | tf_op jit(solution)/shard_map/ppermute | solution.py:726
  4.6 13.4 %collective-permute-start.1 = (f32[64,640]{1,0:T(8,128)S(1)}, f32[64,640]{1,0:T(8,128)S(1)}, u32[]{:S(2)}, u32[]{:S(2)}) collective-permute-start(f32[64,640]{1,0:T(8,128)S(1)} %get-tuple-element.24), channel_id=1, source_target_pairs={{0,65},{1,66},{2,67},{3,64},{4,69},{5,70},{6,71},{7,68},{8,73},{9,... | collective-permute-start | bytes 491528 | tf_op jit(solution)/shard_map/ppermute | solution.py:726
  7.7 10.4 %collective-permute-start.2 = (f32[64,640]{1,0:T(8,128)S(1)}, f32[64,640]{1,0:T(8,128)S(1)}, u32[]{:S(2)}, u32[]{:S(2)}) collective-permute-start(f32[64,640]{1,0:T(8,128)S(1)} %get-tuple-element.25), channel_id=1, source_target_pairs={{0,66},{1,67},{2,64},{3,65},{4,70},{5,71},{6,68},{7,69},{8,74},{9,... | collective-permute-start | bytes 491528 | tf_op jit(solution)/shard_map/ppermute | solution.py:726
  8.1 9.9 %collective-permute-start.3 = (f32[64,640]{1,0:T(8,128)S(1)}, f32[64,640]{1,0:T(8,128)S(1)}, u32[]{:S(2)}, u32[]{:S(2)}) collective-permute-start(f32[64,640]{1,0:T(8,128)S(1)} %get-tuple-element.26), channel_id=1, source_target_pairs={{0,67},{1,64},{2,65},{3,66},{4,71},{5,68},{6,69},{7,70},{8,75},{9,... | collective-permute-start | bytes 491528 | tf_op jit(solution)/shard_map/ppermute | solution.py:726
  18.0 26.4 %copy-start.4 = (f32[2]{0:T(128)S(1)}, f32[2]{0:T(128)}, u32[]{:S(2)}) copy-start(f32[2]{0:T(128)} %geo_ref.1) | copy-start | bytes 28
  18.0 26.4 %copy-start.5 = (bf16[512,256]{1,0:T(8,128)(2,1)S(1)}, bf16[512,256]{1,0:T(8,128)(2,1)}, u32[]{:S(2)}) copy-start(bf16[512,256]{1,0:T(8,128)(2,1)} %constant.36.clone.fold_ref) | copy-start | bytes 786436
  18.0 26.4 %copy-start.6 = (bf16[256,256]{1,0:T(8,128)(2,1)S(1)}, bf16[256,256]{1,0:T(8,128)(2,1)}, u32[]{:S(2)}) copy-start(bf16[256,256]{1,0:T(8,128)(2,1)} %constant.37.clone.unfold_ref) | copy-start | bytes 393220
  18.0 26.4 %copy-start.7 = (bf16[240,256]{1,0:T(8,128)(2,1)S(1)}, bf16[240,256]{1,0:T(8,128)(2,1)}, u32[]{:S(2)}) copy-start(bf16[240,256]{1,0:T(8,128)(2,1)} %constant.35.clone.gather_ref) | copy-start | bytes 368644
  20.9 23.4 %all-to-all-start = ((f32[128,1,1280]{2,1,0:T(1,128)}), f32[128,1,1280]{2,1,0:T(1,128)S(1)}, u32[]{:S(2)}, u32[]{:S(2)}) async-start(f32[128,1,1280]{2,1,0:T(1,128)} %copy.16), calls=%async_computation | async-start | bytes 1310720 | tf_op jit(solution)/shard_map/all_to_all | solution.py:759
  44.4 40.8 %copy-start = (bf16[1024,256]{1,0:T(8,128)(2,1)S(1)}, bf16[1024,256]{1,0:T(8,128)(2,1)}, u32[]{:S(2)}) copy-start(bf16[1024,256]{1,0:T(8,128)(2,1)} %constant.39.clone.table_ref) | copy-start | bytes 1572868
  44.4 40.8 %copy-start.3 = (bf16[160,128]{1,0:T(8,128)(2,1)S(1)}, bf16[160,128]{1,0:T(8,128)(2,1)}, u32[]{:S(2)}) copy-start(bf16[160,128]{1,0:T(8,128)(2,1)} %constant.38.clone.scatter_ref) | copy-start | bytes 122884
  88.1 5.5 %collective-permute-start.4 = (f32[64,640]{1,0:T(8,128)S(1)}, f32[64,640]{1,0:T(8,128)S(1)}, u32[]{:S(2)}, u32[]{:S(2)}) collective-permute-start(f32[64,640]{1,0:T(8,128)S(1)} %get-tuple-element.39), channel_id=1, source_target_pairs={{0,64},{1,65},{2,66},{3,67},{4,68},{5,69},{6,70},{7,71},{8,72},{9,... | collective-permute-start | bytes 491528 | tf_op jit(solution)/shard_map/ppermute | solution.py:726
  88.8 9.2 %collective-permute-start.5 = (f32[64,640]{1,0:T(8,128)S(1)}, f32[64,640]{1,0:T(8,128)S(1)}, u32[]{:S(2)}, u32[]{:S(2)}) collective-permute-start(f32[64,640]{1,0:T(8,128)S(1)} %get-tuple-element.40), channel_id=1, source_target_pairs={{0,65},{1,66},{2,67},{3,64},{4,69},{5,70},{6,71},{7,68},{8,73},{9,... | collective-permute-start | bytes 491528 | tf_op jit(solution)/shard_map/ppermute | solution.py:726
  90.7 8.1 %collective-permute-start.6 = (f32[64,640]{1,0:T(8,128)S(1)}, f32[64,640]{1,0:T(8,128)S(1)}, u32[]{:S(2)}, u32[]{:S(2)}) collective-permute-start(f32[64,640]{1,0:T(8,128)S(1)} %get-tuple-element.41), channel_id=1, source_target_pairs={{0,66},{1,67},{2,64},{3,65},{4,70},{5,71},{6,68},{7,69},{8,74},{9,... | collective-permute-start | bytes 491528 | tf_op jit(solution)/shard_map/ppermute | solution.py:726
  92.0 8.0 %collective-permute-start.7 = (f32[64,640]{1,0:T(8,128)S(1)}, f32[64,640]{1,0:T(8,128)S(1)}, u32[]{:S(2)}, u32[]{:S(2)}) collective-permute-start(f32[64,640]{1,0:T(8,128)S(1)} %get-tuple-element.42), channel_id=1, source_target_pairs={{0,67},{1,64},{2,65},{3,66},{4,71},{5,68},{6,69},{7,70},{8,75},{9,... | collective-permute-start | bytes 491528 | tf_op jit(solution)/shard_map/ppermute | solution.py:726
